TPU v7x, 32 devices: a whole 2x2x4 slice. The times are simulated.
32 devices in a mesh: ent: 8 (over z, y), rep: 4 (over x, core).
Axes of the slice: x: 2, y: 2, z: 4, core: 2. Of those that a mesh axis runs over, the one named last changes fastest.
Arguments:
- memory: bfloat16 [16384, 512], P('ent'), may hold values from -6 to 6
- edge_features: bfloat16 [12288, 128], P(('ent', 'rep')), may hold values from -6 to 6
- source: int32 [12288], P(('ent', 'rep')), may hold values from 0 to 16383, as said below
- target: int32 [12288], P(('ent', 'rep')), may hold values from 0 to 16383, as said below
- cotangent: bfloat16 [12288, 512], P(('ent', 'rep')), may hold values from -6 to 6
- w_first: bfloat16 [1152, 512], replicated, may hold values from -0.1875 to 0.1875
- w_second: bfloat16 [512, 512], replicated, may hold values from -0.25 to 0.25
- w_input: bfloat16 [512, 1536], replicated, may hold values from -0.25 to 0.25
- w_hidden: bfloat16 [512, 1536], replicated, may hold values from -0.25 to 0.25
Outputs:
- memory_grad: float32 [16384, 512], P('ent', 'rep')
- first_grad: float32 [1152, 512], P('ent')
- second_grad: float32 [512, 512], P('ent')
- input_grad: float32 [512, 1536], P('ent')
- hidden_grad: float32 [512, 1536], P('ent')
Inputs may be any that keep to these rules, and one draw needn't show every extreme that they name: `source`: entity ids; an entity is a hub when its id modulo 2048 is below 8, and its owner is its id divided by 2048. In each aligned block of 384 events (the events of one device), sources and targets taken together hold exactly 192 hub endpoints; no owner gets more than 144 non-hub endpoints or more than 240 endpoints in all from one block, and in every draw one owner gets exactly 144 non-hub endpoints and 240 in all from every block. `target`: entity ids under the same rules, counted together with source.
All inputs are finite; a program needn't handle non-finite values.
Results may differ from a plain program's by a relative error of at most 0.0057.
Values may be sent and summed in bfloat16 or wider, within the bound.
No kernel may reach another device: no remote copies, remote signals or barrier semaphores. Data moves between devices by JAX's collectives and lax.ppermute only.
A program may use at most 128 MiB of HBM per device.

v0:
```python
import math

import jax
import jax.numpy as jnp
from jax import lax
from jax.sharding import PartitionSpec as P


def contract_last(left, right):
    return lax.dot_general(
        left, right, (((1,), (1,)), ((), ())), preferred_element_type=jnp.float32
    )


def contract_first(left, right):
    return lax.dot_general(
        left, right, (((0,), (0,)), ((), ())), preferred_element_type=jnp.float32
    )


def event_backward(mem_src, mem_dst, edge_rows, cot_rows, w_first, w_second, w_input, w_hidden):
    mem_width = mem_src.shape[1]
    inputs = jnp.concatenate([mem_src, mem_dst, edge_rows], axis=1)
    pre_hidden = jnp.dot(inputs, w_first, preferred_element_type=jnp.float32)
    hidden = jax.nn.silu(pre_hidden).astype(jnp.bfloat16)
    message = jnp.dot(hidden, w_second, preferred_element_type=jnp.float32).astype(jnp.bfloat16)
    gate_in = jnp.dot(message, w_input, preferred_element_type=jnp.float32)
    gate_mem = jnp.dot(mem_src, w_hidden, preferred_element_type=jnp.float32)
    reset_gate = jax.nn.sigmoid(gate_in[:, :mem_width] + gate_mem[:, :mem_width])
    update = jax.nn.sigmoid(
        gate_in[:, mem_width : 2 * mem_width] + gate_mem[:, mem_width : 2 * mem_width]
    )
    mem_cand = gate_mem[:, 2 * mem_width :]
    candidate = jnp.tanh(gate_in[:, 2 * mem_width :] + reset_gate * mem_cand)
    upstream = cot_rows.astype(jnp.float32)
    pre_cand = upstream * (1.0 - update) * (1.0 - candidate * candidate)
    pre_reset = pre_cand * mem_cand * reset_gate * (1.0 - reset_gate)
    pre_update = upstream * (mem_src.astype(jnp.float32) - candidate) * update * (1.0 - update)
    d_gate_in = jnp.concatenate([pre_reset, pre_update, pre_cand], axis=1).astype(jnp.bfloat16)
    d_gate_mem = jnp.concatenate([pre_reset, pre_update, pre_cand * reset_gate], axis=1).astype(
        jnp.bfloat16
    )
    d_message = contract_last(d_gate_in, w_input).astype(jnp.bfloat16)
    back_hidden = contract_last(d_message, w_second)
    sigma_pre = jax.nn.sigmoid(pre_hidden)
    d_pre = (back_hidden * sigma_pre * (1.0 + pre_hidden * (1.0 - sigma_pre))).astype(jnp.bfloat16)
    d_inputs = contract_last(d_pre, w_first[: 2 * mem_width])
    via_memory = contract_last(d_gate_mem, w_hidden)
    d_source = upstream * update + via_memory + d_inputs[:, :mem_width]
    d_target = d_inputs[:, mem_width:]
    saved_rows = (inputs, d_pre, hidden, d_message, message, d_gate_in, d_gate_mem)
    return (d_source, d_target, saved_rows)


def assign_slots(owner_of, active, owners, capacity):
    owner_ids = jnp.arange(owners, dtype=jnp.int32)
    onehot = jnp.logical_and(owner_of[:, None] == owner_ids[None, :], active[:, None]).astype(
        jnp.int32
    )
    earlier = jnp.cumsum(onehot, axis=0) - onehot
    rank_in = jnp.sum(earlier * onehot, axis=1)
    return owner_of * capacity + rank_in


def per_device(
    memory, edge_features, source, target, cotangent, w_first, w_second, w_input, w_hidden
):
    owners = lax.axis_size("ent")
    replicas = lax.axis_size("rep")
    ent_rows = memory.shape[0]
    mem_width = memory.shape[1]
    events = source.shape[0]
    grad_scale = 1.0 / math.sqrt(events * owners * replicas)
    hub_req = events // 2
    nonhub = 2 * events - hub_req
    cap_rest = 2 * nonhub // owners
    cap_hub = 4 * hub_req // owners
    endpoints = jnp.concatenate([source, target])
    owner_of = endpoints // ent_rows
    local_row = endpoints % ent_rows
    active = jnp.ones(endpoints.shape, jnp.bool_)
    capacity = cap_rest + cap_hub
    slot_index = assign_slots(owner_of, active, owners, capacity)
    slot_target = jnp.where(active, slot_index, owners * capacity)
    send_rows = (
        jnp.zeros((owners * capacity,), jnp.int32).at[slot_target].set(local_row, mode="drop")
    )
    send_rows = send_rows.reshape(owners, capacity)
    asked_rows = lax.all_to_all(send_rows, "ent", split_axis=0, concat_axis=0, tiled=True)
    found_rows = jnp.take(memory, asked_rows, axis=0)
    fetched = lax.all_to_all(found_rows, "ent", split_axis=0, concat_axis=0, tiled=True)
    flat_rows = fetched.reshape(owners * capacity, mem_width)
    gathered = jnp.take(flat_rows, jnp.where(active, slot_index, 0), axis=0)
    mem_src = gathered[:events]
    mem_dst = gathered[events:]
    d_source, d_target, saved_rows = event_backward(
        mem_src, mem_dst, edge_features, cotangent, w_first, w_second, w_input, w_hidden
    )
    inputs, d_pre, hidden, d_message, message, d_gate_in, d_gate_mem = saved_rows
    end_grads = jnp.concatenate([d_source, d_target], axis=0)
    outgoing = (
        jnp.zeros((owners * capacity, mem_width), jnp.float32)
        .at[slot_target]
        .set(end_grads, mode="drop")
    )
    returned = lax.all_to_all(
        outgoing.reshape(owners, capacity, mem_width),
        "ent",
        split_axis=0,
        concat_axis=0,
        tiled=True,
    )
    local_grad = (
        jnp.zeros((ent_rows, mem_width), jnp.float32)
        .at[asked_rows.reshape(-1)]
        .add(returned.reshape(-1, mem_width))
    )
    memory_grad = lax.psum_scatter(local_grad, "rep", scatter_dimension=1, tiled=True)
    first_part = lax.psum_scatter(
        grad_scale * contract_first(inputs, d_pre), "ent", scatter_dimension=0, tiled=True
    )
    rest_part = lax.psum_scatter(
        grad_scale
        * jnp.concatenate(
            [
                contract_first(hidden, d_message),
                contract_first(message, d_gate_in),
                contract_first(mem_src, d_gate_mem),
            ],
            axis=1,
        ),
        "ent",
        scatter_dimension=0,
        tiled=True,
    )
    first_grad, rest_grad = lax.psum((first_part, rest_part), "rep")
    return (
        memory_grad,
        first_grad,
        rest_grad[:, :mem_width],
        rest_grad[:, mem_width : 4 * mem_width],
        rest_grad[:, 4 * mem_width :],
    )


def solution(mesh):
    return jax.shard_map(
        per_device,
        mesh=mesh,
        in_specs=(
            P("ent", None),
            P(("ent", "rep"), None),
            P(("ent", "rep")),
            P(("ent", "rep")),
            P(("ent", "rep"), None),
            P(),
            P(),
            P(),
            P(),
        ),
        out_specs=(P("ent", "rep"), P("ent", None), P("ent", None), P("ent", None), P("ent", None)),
        check_vma=False,
    )
```

profile of v0, /device:TPU:0, one launch (start us, length us, event | category | flops | bytes accessed | tf_op | source)
XLA Modules:
  0.0 462.5 jit_solution(15237524545849237657)
XLA Ops:
  7.2 0.8 constant_dynamic-update-slice_fusion.2
  8.8 1.7 reduce-window.6
  12.4 3.4 scatter_custom_fusion
  15.9 13.6 %all_to_all.25 = s32[8,1,240]{2,1,0:T(1,128)S(1)} all-to-all(s32[8,1,240]{2,1,0:T(1,128)S(1)} %all_to_all.16), channel_id=1, replica_groups=mesh['ent'=8,'rep'=4] {'ent'}, dimensions={0} | all-to-all | bytes 15360 | tf_op jit(solution)/shard_map/all_to_all | solution.py:89
  29.7 6.8 %gather_fusion = bf16[1920,512]{1,0:T(8,128)(2,1)} fusion(bf16[2048,512]{1,0:T(8,128)(2,1)S(1)} %copy-done, s32[2048]{0:T(1024)S(1)} %pad_clamp_fusion), kind=kCustom, calls=%fused_computation | custom fusion | bytes 3939840 | tf_op jit(solution)/shard_map/jit(_take)/gather | solution.py:90
  36.5 2.7 broadcast_select_fusion
  39.2 4.4 all-to-all-start.1
  43.7 44.2 %all-to-all-done.1 = bf16[8,240,512]{2,1,0:T(8,128)(2,1)} async-done(((bf16[8,240,512]{2,1,0:T(8,128)(2,1)}), bf16[8,240,512]{2,1,0:T(8,128)(2,1)}, u32[]{:S(2)}, u32[]{:S(2)}) %all-to-all-start.1) | async-done | bytes 1966112 | tf_op jit(solution)/shard_map/all_to_all | solution.py:91
  87.9 5.2 %gather_fusion.1 = bf16[768,512]{1,0:T(8,128)(2,1)} fusion(bf16[1920,512]{1,0:T(8,128)(2,1)} %bitcast.5, s32[1024]{0:T(1024)S(1)} %pad_clamp_fusion.1), kind=kCustom, calls=%fused_computation.1 | custom fusion | bytes 1575936 | tf_op jit(solution)/shard_map/jit(_take)/gather | solution.py:93
  93.0 1.4 broadcast_select_fusion.1
  94.7 0.8 fusion.48
  97.7 1.3 copy-done.14
  99.0 0.8 fusion.55
  100.2 1.5 multiply_convert_fusion
  102.4 0.8 convolution_convert_fusion.1
  104.8 2.2 convolution_multiply_fusion
  107.3 1.8 fusion.50
  109.2 1.0 fusion.25
  110.2 1.0 fusion.26
  111.2 3.4 maximum_multiply_fusion
  114.6 1.0 copy-done.19
  115.6 2.0 fusion.10
  117.7 3.2 fusion.8
  120.9 8.6 %scatter_custom_fusion.1 = f32[1920,512]{1,0:T(8,128)} fusion(s32[768]{0:T(1024)S(1)} %fusion.39, f32[]{:T(128)} %constant.50.clone.1, f32[384,512]{1,0:T(8,128)S(1)} %slice.78, f32[]{:T(128)} %constant.83, f32[384,512]{1,0:T(8,128)} %fusion.8), kind=kCustom, calls=%fused_computation.9 | custom fusion | flops 393216 | bytes 5505032 | tf_op jit(solution)/shard_map/scatter | solution.py:104
  129.4 4.5 all-to-all-start.2
  134.0 94.7 %reduce-scatter.6.cloned.1.call-done = f32[144,512]{1,0:T(8,128)} async-done(((f32[1152,512]{1,0:T(8,128)}), f32[144,512]{1,0:T(8,128)}) %reduce-scatter.6.cloned.1.call-update) | async-done | bytes 294928 | tf_op jit(solution)/shard_map/reduce_scatter | solution.py:119
  228.7 139.7 %reduce-scatter.8.cloned.1.call-done = f32[64,3584]{1,0:T(8,128)} async-done(((f32[512,3584]{1,0:T(8,128)}), f32[64,3584]{1,0:T(8,128)}) %reduce-scatter.8.cloned.1.call-update) | async-done | bytes 917520 | tf_op jit(solution)/shard_map/reduce_scatter | solution.py:122
  368.6 16.8 %scatter_custom_fusion.2 = f32[2048,512]{1,0:T(8,128)} fusion(s32[1920]{0:T(1024)S(1)} %fusion.32, f32[1920,512]{1,0:T(8,128)} %bitcast.7, f32[]{:T(128)} %constant.50.clone.1), kind=kCustom, calls=%fused_computation.7 | custom fusion | flops 983040 | bytes 4194816 | tf_op jit(solution)/shard_map/scatter-add | solution.py:116
  385.5 22.4 %all-reduce.3.cloned.1.call-done = (f32[144,512]{1,0:T(8,128)}, f32[64,3584]{1,0:T(8,128)}) async-done(((f32[144,512]{1,0:T(8,128)}, f32[64,3584]{1,0:T(8,128)}), (f32[144,512]{1,0:T(8,128)}, f32[64,3584]{1,0:T(8,128)})) %all-reduce.3.cloned.1.call-update) | async-done | bytes 1212432 | tf_op jit(solution)/shard_map/psum | solution.py:136
  407.9 1.6 slice.79
  409.5 2.0 fusion.53
  411.5 43.8 %reduce-scatter.4.cloned.1.call-done = f32[2048,128]{1,0:T(8,128)} async-done(((f32[2048,512]{1,0:T(8,128)}), f32[2048,128]{1,0:T(8,128)}) %reduce-scatter.4.cloned.1.call-update) | async-done | bytes 1048592 | tf_op jit(solution)/shard_map/reduce_scatter | solution.py:118
  (88 shorter events, 9.4 us)
Async XLA Ops:
  7.2 22.5 %copy-start = (bf16[2048,512]{1,0:T(8,128)(2,1)S(1)}, bf16[2048,512]{1,0:T(8,128)(2,1)}, u32[]{:S(2)}) copy-start(bf16[2048,512]{1,0:T(8,128)(2,1)} %param.9) | copy-start | bytes 6291460
  39.2 48.6 %all-to-all-start.1 = ((bf16[8,240,512]{2,1,0:T(8,128)(2,1)}), bf16[8,240,512]{2,1,0:T(8,128)(2,1)}, u32[]{:S(2)}, u32[]{:S(2)}) async-start(bf16[8,240,512]{2,1,0:T(8,128)(2,1)} %broadcast_select_fusion), calls=%async_computation.1 | async-start | bytes 3932160 | tf_op jit(solution)/shard_map/all_to_all | solution.py:91
  43.6 185.1 %reduce-scatter.6.cloned.1.call-start = ((), (), s32[]{:S(2)}) async-start(), calls=%async_computation.7 | async-start | bytes 2654208 | tf_op jit(solution)/shard_map/reduce_scatter | solution.py:119
  93.0 1.6 copy-start.15
  94.7 1.3 copy-start.17
  94.7 1.3 copy-start.22
  95.5 6.2 %copy-start.1 = (f32[384,1536]{1,0:T(8,128)}, f32[384,1536]{1,0:T(8,128)S(1)}, u32[]{:S(2)}) copy-start(f32[384,1536]{1,0:T(8,128)S(1)} %fusion.48) | copy-start | bytes 7077892
  95.9 1.4 copy-start.21
  97.3 5.9 %copy-start.23 = (f32[384,512]{1,0:T(8,128)}, f32[384,512]{1,0:T(8,128)S(1)}, u32[]{:S(2)}) copy-start(f32[384,512]{1,0:T(8,128)S(1)} %fusion.27) | copy-start | bytes 2359300
  97.3 1.7 copy-start.14
  99.0 0.8 copy-start.6
  99.0 1.1 copy-start.8
  100.2 1.5 copy-start.2
  102.4 0.8 copy-start.3
  102.4 0.9 copy-start.12
  103.3 0.8 copy-start.24
  104.1 0.7 copy-start.18
  107.0 261.4 %reduce-scatter.8.cloned.1.call-start = ((), (), s32[]{:S(2)}) async-start(), calls=%async_computation.8 | async-start | bytes 8257536 | tf_op jit(solution)/shard_map/reduce_scatter | solution.py:122
  107.3 1.9 copy-start.4
  107.3 1.9 copy-start.7
  107.3 1.9 copy-start.13
  109.2 1.0 copy-start.10
  114.6 1.0 copy-start.19
  115.6 2.1 copy-start.5
  115.6 2.1 copy-start.9
  115.6 2.1 copy-start.11
  115.6 2.1 copy-start.16
  129.4 239.2 %all-to-all-start.2 = ((f32[8,240,512]{2,1,0:T(8,128)}), f32[8,240,512]{2,1,0:T(8,128)}, u32[]{:S(2)}, u32[]{:S(2)}) async-start(f32[8,240,512]{2,1,0:T(8,128)} %bitcast.49), calls=%async_computation.2 | async-start | bytes 7864320 | tf_op jit(solution)/shard_map/all_to_all | solution.py:106
  133.9 273.9 %all-reduce.3.cloned.1.call-start = ((), (), s32[]{:S(2)}) async-start(), calls=%async_computation.9 | async-start | bytes 2424832 | tf_op jit(solution)/shard_map/psum | solution.py:136
  368.4 86.9 %reduce-scatter.4.cloned.1.call-start = ((), (), s32[]{:S(2)}) async-start(), calls=%async_computation.6 | async-start | bytes 5242880 | tf_op jit(solution)/shard_map/reduce_scatter | solution.py:118
  407.9 47.4 %copy-start.20 = (f32[144,512]{1,0:T(8,128)S(1)}, f32[144,512]{1,0:T(8,128)}, u32[]{:S(2)}) copy-start(f32[144,512]{1,0:T(8,128)} %get-tuple-element.20) | copy-start | bytes 884740
Sparse Core Ops, SparseCore 0:
  107.2 121.4 reduce-scatter.5
  232.3 136.0 reduce-scatter.7
  370.8 36.9 all-reduce.2
  410.8 44.4 reduce-scatter.3
where the time goes:
time: 463 us
  waiting for transfers between devices  345 us (75%)
  other arithmetic  37.3 us (8%)
  local copies, waits for them, and re-layouts  28.4 us (6%)
  matrix products  15.1 us (3%)
  between operations  14.1 us (3%)
  blocking collectives  13.6 us (3%)
  starting transfers between devices  9.22 us (2%)
    reduce_scatter x1, waiting for transfers between devices, per_device(): lax.psum_scatter(grad_scale * jnp.concatenate([contract_first(hidden, d_m...  140 us
    reduce_scatter x1, waiting for transfers between devices, per_device(): lax.psum_scatter(grad_scale * contract_first(inputs, d_pre), 'ent', scatt...  94.7 us
    all_to_all x1, waiting for transfers between devices, per_device(): lax.all_to_all(found_rows, 'ent', split_axis=0, concat_axis=0, tiled=True)  44.2 us
    reduce_scatter x1, waiting for transfers between devices, per_device(): lax.psum_scatter(local_grad, 'rep', scatter_dimension=1, tiled=True)  43.8 us
    psum x1, waiting for transfers between devices, per_device(): first_grad, rest_grad = lax.psum((first_part, rest_part), 'rep')  22.4 us
    scatter-add x1, other arithmetic, per_device(): local_grad = jnp.zeros((ent_rows, mem_width), jnp.float32).at[asked_rows....  16.8 us
    all_to_all x1, blocking collectives, per_device(): lax.all_to_all(send_rows, 'ent', split_axis=0, concat_axis=0, tiled=True)  13.6 us
  transfers between devices with their start and end apart: 6, of which 5 were waited for; matrix products, arithmetic and copies ran while one was open for 9% of the time, Pallas kernels for 0%

commit v1 on v0

v1 whole, which is shorter than its diff:
```python
import functools
import math

import jax
import jax.numpy as jnp
from jax import lax
from jax.experimental import pallas as pl
from jax.experimental.pallas import tpu as pltpu
from jax.sharding import PartitionSpec as P

HUBS = 8
BF16 = jnp.bfloat16
F32 = jnp.float32


def contract_last(left, right):
    return lax.dot_general(left, right, (((1,), (1,)), ((), ())), preferred_element_type=F32)


def contract_first(left, right):
    return lax.dot_general(left, right, (((0,), (0,)), ((), ())), preferred_element_type=F32)


def swap_bit(value, axis, bit):
    size = lax.axis_size(axis)
    return lax.ppermute(value, axis, [(i, i ^ (1 << bit)) for i in range(size)])


def forward_gates(mem_src, mem_dst, edge_rows, cot_rows, w_first, w_second, w_input, w_hidden):
    width = mem_src.shape[1]
    inputs = jnp.concatenate([mem_src, mem_dst, edge_rows], axis=1)
    pre_hidden = jnp.dot(inputs, w_first, preferred_element_type=F32)
    hidden = jax.nn.silu(pre_hidden).astype(BF16)
    message = jnp.dot(hidden, w_second, preferred_element_type=F32).astype(BF16)
    gate_in = jnp.dot(message, w_input, preferred_element_type=F32)
    gate_mem = jnp.dot(mem_src, w_hidden, preferred_element_type=F32)
    reset_gate = jax.nn.sigmoid(gate_in[:, :width] + gate_mem[:, :width])
    update = jax.nn.sigmoid(gate_in[:, width : 2 * width] + gate_mem[:, width : 2 * width])
    mem_cand = gate_mem[:, 2 * width :]
    candidate = jnp.tanh(gate_in[:, 2 * width :] + reset_gate * mem_cand)
    upstream = cot_rows.astype(F32)
    pre_cand = upstream * (1.0 - update) * (1.0 - candidate * candidate)
    pre_reset = pre_cand * mem_cand * reset_gate * (1.0 - reset_gate)
    pre_update = upstream * (mem_src.astype(F32) - candidate) * update * (1.0 - update)
    d_gate_in = jnp.concatenate([pre_reset, pre_update, pre_cand], axis=1).astype(BF16)
    d_gate_mem = jnp.concatenate([pre_reset, pre_update, pre_cand * reset_gate], axis=1).astype(BF16)
    return inputs, pre_hidden, hidden, message, upstream * update, d_gate_in, d_gate_mem


def scatter_kernel(block, idx_ref, val_ref, out_ref):
    rows = pl.program_id(0) * block + lax.broadcasted_iota(jnp.int32, (block, idx_ref.shape[1]), 0)
    pick = jnp.where(rows == idx_ref[...], 1.0, 0.0).astype(BF16)
    out_ref[...] = jnp.dot(pick, val_ref[...], preferred_element_type=F32)


def scatter_rows(index, values, rows):
    count, width = values.shape
    block = 256
    return pl.pallas_call(
        functools.partial(scatter_kernel, block),
        out_shape=jax.ShapeDtypeStruct((rows, width), F32),
        grid=(rows // block,),
        in_specs=[
            pl.BlockSpec((1, count), lambda i: (0, 0)),
            pl.BlockSpec((count, width), lambda i: (0, 0)),
        ],
        out_specs=pl.BlockSpec((block, width), lambda i: (i, 0)),
        cost_estimate=pl.CostEstimate(
            flops=2 * rows * count * width,
            bytes_accessed=count * width * 2 + rows * width * 4,
            transcendentals=0,
        ),
    )(index.reshape(1, count), values)


def per_device(
    memory, edge_features, source, target, cotangent, w_first, w_second, w_input, w_hidden
):
    owners = lax.axis_size("ent")
    replicas = lax.axis_size("rep")
    rep = lax.axis_index("rep")
    ent = lax.axis_index("ent")
    rep_bits = replicas.bit_length() - 1
    ent_bits = owners.bit_length() - 1
    ent_rows, width = memory.shape
    events = source.shape[0]
    grad_scale = 1.0 / math.sqrt(events * owners * replicas)
    hub_req = events // 2
    nonhub = 2 * events - hub_req
    cap = 2 * nonhub // owners
    slots = cap + HUBS

    endpoints = jnp.concatenate([source, target])
    owner_of = endpoints // ent_rows
    local_row = endpoints % ent_rows
    is_hub = local_row < HUBS
    member = jnp.logical_and(
        owner_of[:, None] == jnp.arange(owners, dtype=jnp.int32)[None, :], ~is_hub[:, None]
    )
    place = jnp.arange(2 * events, dtype=jnp.int32)
    before = (place[None, :] < place[:, None]).astype(BF16)
    earlier = jnp.dot(before, member.astype(BF16), preferred_element_type=F32)
    rank = jnp.sum(jnp.where(member, earlier, 0.0), axis=1).astype(jnp.int32)
    slot = owner_of * slots + jnp.where(is_hub, cap + local_row, rank)
    chosen = slot[:, None] == jnp.arange(owners * slots, dtype=jnp.int32)[None, :]
    pick = chosen.astype(BF16)
    wanted = jnp.sum(jnp.where(chosen, local_row[:, None], 0), axis=0).reshape(owners, slots)
    wanted = wanted[:, :cap]

    asked = lax.all_to_all(wanted.reshape(owners, 1, cap), "ent", 0, 0, tiled=True)
    asked = asked.reshape(owners, cap)
    hub_ids = jnp.broadcast_to(jnp.arange(HUBS, dtype=jnp.int32)[None, :], (owners, HUBS))
    asked = jnp.concatenate([asked, hub_ids], axis=1)
    rows_of = asked.reshape(-1)[:, None] == jnp.arange(ent_rows, dtype=jnp.int32)[None, :]
    found = jnp.dot(rows_of.astype(BF16), memory, preferred_element_type=F32).astype(BF16)
    fetched = lax.all_to_all(found.reshape(owners, slots, width), "ent", 0, 0, tiled=True)
    gathered = jnp.dot(
        pick, fetched.reshape(owners * slots, width), preferred_element_type=F32
    ).astype(BF16)

    asked_all = asked[None]
    for bit in range(rep_bits):
        other = swap_bit(asked_all, "rep", bit)
        upper = (rep >> bit) & 1
        asked_all = jnp.where(
            upper == 1,
            jnp.concatenate([other, asked_all], axis=0),
            jnp.concatenate([asked_all, other], axis=0),
        )
    index = jnp.transpose(asked_all, (1, 0, 2)).reshape(-1)

    mem_src = gathered[:events]
    inputs, pre_hidden, hidden, message, direct, d_gate_in, d_gate_mem = forward_gates(
        mem_src, gathered[events:], edge_features, cotangent, w_first, w_second, w_input, w_hidden
    )
    d_message = contract_last(d_gate_in, w_input).astype(BF16)
    back_hidden = contract_last(d_message, w_second)
    sigma_pre = jax.nn.sigmoid(pre_hidden)
    d_pre = (back_hidden * sigma_pre * (1.0 + pre_hidden * (1.0 - sigma_pre))).astype(BF16)
    d_inputs = contract_last(d_pre, w_first[: 2 * width])
    d_source = direct + contract_last(d_gate_mem, w_hidden) + d_inputs[:, :width]
    end_grads = jnp.concatenate([d_source, d_inputs[:, width:]], axis=0).astype(BF16)

    part = width // replicas
    outgoing = contract_first(pick, end_grads).astype(BF16)
    outgoing = outgoing.reshape(owners, slots, replicas, part).transpose(0, 2, 1, 3)
    returned = lax.all_to_all(
        outgoing.reshape(owners * replicas, slots, part), ("ent", "rep"), 0, 0, tiled=True
    )
    memory_grad = scatter_rows(index, returned.reshape(-1, part), ent_rows)

    def quarter(pairs, which):
        pieces = []
        for left, right in pairs:
            cols = right.shape[1] // replicas
            piece = lax.dynamic_slice_in_dim(right, which * cols, cols, axis=1)
            pieces.append(
                (grad_scale * contract_first(left, piece)).reshape(owners, left.shape[1] // owners, cols)
            )
        return pieces

    def halve_rep(make):
        total = None
        pending = [jnp.int32(0)]
        flips = [0]
        arrived = None
        for bit in range(rep_bits):
            later = [f for f in range(replicas) if f & (1 << bit) and not f & ((1 << bit) - 1)]
            send = []
            for flip in later:
                value = make(rep ^ flip)
                if arrived is not None:
                    value = value + arrived[flip].astype(F32)
                send.append(value.astype(BF16))
            got = swap_bit(jnp.stack(send), "rep", bit)
            fresh = {}
            for place_, flip in enumerate(later):
                base = flip ^ (1 << bit)
                value = got[place_].astype(F32)
                if arrived is not None:
                    value = value + arrived[base]
                fresh[base] = value
            arrived = fresh
        return make(rep) + arrived[0]

    def halve_ent(value):
        for bit in range(ent_bits):
            upper = (ent >> bit) & 1
            shape = value.shape
            pairs = value.reshape((shape[0] // 2, 2) + shape[1:])
            keep = jnp.where(upper == 1, pairs[:, 1], pairs[:, 0])
            send = jnp.where(upper == 1, pairs[:, 0], pairs[:, 1]).astype(BF16)
            value = keep + swap_bit(send, "ent", bit).astype(F32)
        return value[0]

    def spread_rep(value):
        value = value.astype(BF16)[None]
        for bit in range(rep_bits):
            other = swap_bit(value, "rep", bit)
            upper = (rep >> bit) & 1
            value = jnp.where(
                upper == 1,
                jnp.concatenate([other, value], axis=0),
                jnp.concatenate([value, other], axis=0),
            )
        return value.astype(F32)

    def make_gate(which):
        return jnp.concatenate(
            quarter(((message, d_gate_in), (mem_src, d_gate_mem)), which), axis=2
        )

    def make_first(which):
        return jnp.concatenate(quarter(((inputs, d_pre), (hidden, d_message)), which), axis=1)

    gate_sum = spread_rep(halve_ent(halve_rep(make_gate)))
    first_sum = spread_rep(halve_ent(halve_rep(make_first)))

    def columns(value):
        return jnp.transpose(value, (1, 0, 2)).reshape(value.shape[1], -1)

    first_rows = inputs.shape[1] // owners
    gate_cols = 3 * width // replicas
    return (
        memory_grad,
        columns(first_sum[:, :first_rows]),
        columns(first_sum[:, first_rows:]),
        columns(gate_sum[:, :, :gate_cols]),
        columns(gate_sum[:, :, gate_cols:]),
    )


def solution(mesh):
    return jax.shard_map(
        per_device,
        mesh=mesh,
        in_specs=(
            P("ent", None),
            P(("ent", "rep"), None),
            P(("ent", "rep")),
            P(("ent", "rep")),
            P(("ent", "rep"), None),
            P(),
            P(),
            P(),
            P(),
        ),
        out_specs=(P("ent", "rep"), P("ent", None), P("ent", None), P("ent", None), P("ent", None)),
        check_vma=False,
    )
```

time: 463 us -> 167 us (0.36)
  waiting for transfers between devices: 345 us -> 78.7 us
  other arithmetic: 37.3 us -> 7.64 us
  local copies, waits for them, and re-layouts: 28.4 us -> 11.7 us
  between operations: 14.1 us -> 1.32 us
  starting transfers between devices: 9.22 us -> 20.8 us
  matrix products: 15.1 us -> 23.7 us
  Pallas kernels: 0 us -> 8.44 us
    reduce_scatter x3 -> x0, waiting for transfers between devices: 278 us -> none  [the longest x1 140 us: per_device(): lax.psum_scatter(grad_scale * jnp.concatenate([contract_first(hidden, d_m...]
    ppermute x0 -> x16, waiting for transfers between devices: none -> 51 us  [swap_bit(): return lax.ppermute(value, axis, [(i, i ^ 1 << bit) for i in range(size)])]
    psum x1 -> x0, waiting for transfers between devices: 22.4 us -> none  [per_device(): first_grad, rest_grad = lax.psum((first_part, rest_part), 'rep')]
    scatter-add x1 -> x0, other arithmetic: 16.8 us -> none  [per_device(): local_grad = jnp.zeros((ent_rows, mem_width), jnp.float32).at[asked_rows....]
    all_to_all x2, waiting for transfers between devices: 44.2 us -> 27.7 us  [the longest x1 27.7 us: per_device(): lax.all_to_all(found.reshape(owners, slots, width), 'ent', 0, 0, tiled=True)]
    ppermute x0 -> x16, starting transfers between devices: none -> 12.7 us  [swap_bit(): return lax.ppermute(value, axis, [(i, i ^ 1 << bit) for i in range(size)])]
    gather x2 -> x0, local copies, waits for them, and re-layouts: 11.9 us -> none  [the longest x1 6.78 us: per_device(): found_rows = jnp.take(memory, asked_rows, axis=0)]
    scatter x1 -> x0, other arithmetic: 8.55 us -> none  [per_device(): outgoing = jnp.zeros((owners * capacity, mem_width), jnp.float32).at[slot...]
  transfers between devices with their start and end apart: 6 -> 18, of which waited for: 5 -> 10; matrix products, arithmetic and copies ran while one was open for 9% -> 20% of each run, Pallas kernels for 0% -> 5%
where the time goes in v1:
time: 167 us; the launch traced here: 166 us
  waiting for transfers between devices  78.7 us (47%)
  matrix products  23.7 us (14%)
  starting transfers between devices  20.8 us (12%)
  blocking collectives  13.6 us (8%)
  local copies, waits for them, and re-layouts  11.7 us (7%)
  Pallas kernels  8.44 us (5%)
  other arithmetic  7.64 us (5%)
    ppermute x16, waiting for transfers between devices, swap_bit(): return lax.ppermute(value, axis, [(i, i ^ 1 << bit) for i in range(size)])  51 us
    all_to_all x1, waiting for transfers between devices, per_device(): lax.all_to_all(found.reshape(owners, slots, width), 'ent', 0, 0, tiled=True)  27.7 us
    all_to_all x1, blocking collectives, per_device(): lax.all_to_all(wanted.reshape(owners, 1, cap), 'ent', 0, 0, tiled=True)  13.6 us
    ppermute x16, starting transfers between devices, swap_bit(): return lax.ppermute(value, axis, [(i, i ^ 1 << bit) for i in range(size)])  12.7 us
    dot_general x17, matrix products, contract_first(): lax.dot_general(left, right, (((0,), (0,)), ((), ())), preferred_element_...  10.2 us
    pallas_call x1, Pallas kernels, scatter_rows(): pl.pallas_call(functools.partial(scatter_kernel, block), out_shape=jax.Sh...  8.44 us
    all_to_all x1, starting transfers between devices, per_device(): lax.all_to_all(found.reshape(owners, slots, width), 'ent', 0, 0, tiled=True)  4.57 us
    dot_general x1, matrix products, per_device(): jnp.dot(rows_of.astype(BF16), memory, preferred_element_type=F32)  3.85 us
  transfers between devices with their start and end apart: 18, of which 10 were waited for; matrix products, arithmetic and copies ran while one was open for 20% of the time, Pallas kernels for 5%

profile of v1, /device:TPU:0, one launch (start us, length us, event | category | flops | bytes accessed | tf_op | source)
XLA Modules:
  0.0 166.1 jit_solution(8227293406418086400)
XLA Ops:
  3.1 13.6 %all_to_all.15 = s32[8,1,144]{2,1,0:T(1,128)S(1)} all-to-all(s32[8,1,144]{2,1,0:T(1,128)S(1)} %reshape.542), channel_id=1, replica_groups=mesh['ent'=8,'rep'=4] {'ent'}, dimensions={0} | all-to-all | bytes 9216 | tf_op jit(solution)/shard_map/all_to_all | solution.py:110
  16.9 3.9 %fusion.4 = bf16[1216,512]{1,0:T(8,128)(2,1)} fusion(bf16[2048,512]{1,0:T(8,128)(2,1)S(1)} %copy-done, s32[1216]{0:T(1024)S(1)} %eq.40), kind=kOutput, calls=%fused_computation.7 | convolution fusion | flops 2553249792 | bytes 3347200 | tf_op jit(solution)/shard_map/dot_general | solution.py:115
  20.8 4.6 %all-to-all-start.1 = ((bf16[8,152,512]{2,1,0:T(8,128)(2,1)}), bf16[8,152,512]{2,1,0:T(8,128)(2,1)}, u32[]{:S(2)}, u32[]{:S(2)}) async-start(bf16[8,152,512]{2,1,0:T(8,128)(2,1)} %bitcast.2), calls=%async_computation.1 | async-start | bytes 2490368 | tf_op jit(solution)/shard_map/all_to_all | solution.py:116
  26.5 27.7 %all-to-all-done.1 = bf16[8,152,512]{2,1,0:T(8,128)(2,1)} async-done(((bf16[8,152,512]{2,1,0:T(8,128)(2,1)}), bf16[8,152,512]{2,1,0:T(8,128)(2,1)}, u32[]{:S(2)}, u32[]{:S(2)}) %all-to-all-start.1) | async-done | bytes 1245216 | tf_op jit(solution)/shard_map/all_to_all | solution.py:116
  54.2 2.6 %fusion.12 = bf16[768,512]{0,1:T(8,128)(2,1)S(1)} fusion(bf16[1216,512]{1,0:T(8,128)(2,1)} %bitcast.3, s32[768]{0:T(1024)S(1)} %select_add_fusion), kind=kOutput, calls=%fused_computation.24 | convolution fusion | flops 957628416 | bytes 2034688 | tf_op jit(solution)/shard_map/dot_general | solution.py:117
  56.9 1.3 copy-done.6
  61.1 1.0 fusion.115
  70.7 1.3 fusion.15
  72.2 1.6 collective-permute-start.3
  74.6 2.2 %fusion.5 = bf16[1216,512]{1,0:T(8,128)(2,1)} fusion(s32[768]{0:T(1024)S(1)} %select_add_fusion, bf16[384,512]{0,1:T(8,128)(2,1)S(1)} %slice.288, bf16[384,512]{0,1:T(8,128)(2,1)S(1)} %fusion.15), kind=kOutput, calls=%fused_computation.8 | convolution fusion | flops 959430656 | bytes 2034688 | tf_op jit(solution)/shard_map/dot_general | solution.py:21
  76.8 7.6 %collective-permute-done.3 = bf16[1,8,208,128]{3,2,1,0:T(8,128)(2,1)S(1)} collective-permute-done((bf16[1,8,208,128]{3,2,1,0:T(8,128)(2,1)S(1)}, bf16[1,8,208,128]{3,2,1,0:T(8,128)(2,1)S(1)}, u32[]{:S(2)}, u32[]{:S(2)}) %collective-permute-start.3) | collective-permute-done | bytes 426016 | tf_op jit(solution)/shard_map/ppermute | solution.py:26
  84.7 1.3 collective-permute-start.4
  86.0 1.3 convolution_multiply_fusion.11
  87.3 4.2 %collective-permute-done.4 = bf16[4,208,128]{2,1,0:T(8,128)(2,1)S(1)} collective-permute-done((bf16[4,208,128]{2,1,0:T(8,128)(2,1)S(1)}, bf16[4,208,128]{2,1,0:T(8,128)(2,1)S(1)}, u32[]{:S(2)}, u32[]{:S(2)}) %collective-permute-start.4) | collective-permute-done | bytes 213024 | tf_op jit(solution)/shard_map/ppermute | solution.py:26
  91.7 1.3 fusion.11
  93.1 1.5 collective-permute-start.10
  94.7 1.3 convolution_multiply_fusion.10
  96.1 2.6 %reshape.546 = bf16[8,152,4,128]{3,2,1,0:T(4,128)(2,1)S(1)} reshape(bf16[1216,512]{1,0:T(8,128)(2,1)} %fusion.5) | data formatting | bytes 2490368 | tf_op jit(solution)/shard_map/reshape | solution.py:146
  98.7 1.2 copy.187
  99.9 3.5 %all-to-all-start.2 = ((bf16[32,152,128]{2,1,0:T(8,128)(2,1)}), bf16[32,152,128]{2,1,0:T(8,128)(2,1)}, u32[]{:S(2)}, u32[]{:S(2)}) async-start(bf16[32,152,128]{2,1,0:T(8,128)(2,1)} %bitcast.5), calls=%async_computation.2 | async-start | bytes 2490368 | tf_op jit(solution)/shard_map/all_to_all | solution.py:147
  103.5 2.7 %collective-permute-start.6 = (bf16[1,208,128]{2,1,0:T(8,128)(2,1)S(1)}, bf16[1,208,128]{2,1,0:T(8,128)(2,1)S(1)}, u32[]{:S(2)}, u32[]{:S(2)}) collective-permute-start(bf16[1,208,128]{2,1,0:T(8,128)(2,1)S(1)} %fusion.79), channel_id=1, source_target_pairs={{0,16},{4,20},{8,24},{12,28},{16,0},{20,4},{24,8},{28,12},{1,17},{... | collective-permute-start | bytes 159752 | tf_op jit(solution)/shard_map/ppermute | solution.py:26
  106.2 14.2 %collective-permute-done.10 = bf16[1,8,64,768]{3,2,1,0:T(8,128)(2,1)} collective-permute-done((bf16[1,8,64,768]{3,2,1,0:T(8,128)(2,1)}, bf16[1,8,64,768]{3,2,1,0:T(8,128)(2,1)}, u32[]{:S(2)}, u32[]{:S(2)}) %collective-permute-start.10) | collective-permute-done | bytes 786464 | tf_op jit(solution)/shard_map/ppermute | solution.py:26
  120.4 1.5 convert_add_fusion
  122.2 1.3 collective-permute-start.11
  123.6 12.4 %collective-permute-done.6 = bf16[1,208,128]{2,1,0:T(8,128)(2,1)S(1)} collective-permute-done((bf16[1,208,128]{2,1,0:T(8,128)(2,1)S(1)}, bf16[1,208,128]{2,1,0:T(8,128)(2,1)S(1)}, u32[]{:S(2)}, u32[]{:S(2)}) %collective-permute-start.6) | collective-permute-done | bytes 53280 | tf_op jit(solution)/shard_map/ppermute | solution.py:26
  136.9 1.5 collective-permute-start.1
  139.3 1.4 collective-permute-done.1
  141.4 2.2 %collective-permute-done.8 = bf16[2,208,128]{2,1,0:T(8,128)(2,1)S(1)} collective-permute-done((bf16[2,208,128]{2,1,0:T(8,128)(2,1)S(1)}, bf16[2,208,128]{2,1,0:T(8,128)(2,1)S(1)}, u32[]{:S(2)}, u32[]{:S(2)}) %collective-permute-start.8) | collective-permute-done | bytes 106528 | tf_op jit(solution)/shard_map/ppermute | solution.py:26
  143.6 2.4 %collective-permute-done.12 = bf16[2,64,768]{2,1,0:T(8,128)(2,1)S(1)} collective-permute-done((bf16[2,64,768]{2,1,0:T(8,128)(2,1)S(1)}, bf16[2,64,768]{2,1,0:T(8,128)(2,1)S(1)}, u32[]{:S(2)}, u32[]{:S(2)}) %collective-permute-start.12) | collective-permute-done | bytes 196640 | tf_op jit(solution)/shard_map/ppermute | solution.py:26
  146.9 6.0 %collective-permute-done.13 = bf16[1,64,768]{2,1,0:T(8,128)(2,1)S(1)} collective-permute-done((bf16[1,64,768]{2,1,0:T(8,128)(2,1)S(1)}, bf16[1,64,768]{2,1,0:T(8,128)(2,1)S(1)}, u32[]{:S(2)}, u32[]{:S(2)}) %collective-permute-start.13) | collective-permute-done | bytes 98336 | tf_op jit(solution)/shard_map/ppermute | solution.py:26
  154.4 1.5 collective-permute-start.15
  155.9 8.4 %shard_map.128 = f32[2048,128]{1,0:T(8,128)} custom-call(s32[1,4864]{1,0:T(1,128)} %reshape_reshape.3.idx_ref, bf16[4864,128]{1,0:T(8,128)(2,1)} %bitcast.6.val_ref), custom_call_target="tpu_custom_call" | custom-call | flops 2550136832 | bytes 2293760 | tf_op jit(solution)/shard_map/pallas_call | solution.py:59
  (114 shorter events, 23.4 us)
Async XLA Ops:
  0.6 16.3 %copy-start = (bf16[2048,512]{1,0:T(8,128)(2,1)S(1)}, bf16[2048,512]{1,0:T(8,128)(2,1)}, u32[]{:S(2)}) copy-start(bf16[2048,512]{1,0:T(8,128)(2,1)} %param.9) | copy-start | bytes 6291460
  20.8 4.6 %copy-start.10 = (bf16[384,128]{1,0:T(8,128)(2,1)S(1)}, bf16[384,128]{1,0:T(8,128)(2,1)}, u32[]{:S(2)}) copy-start(bf16[384,128]{1,0:T(8,128)(2,1)} %param.10) | copy-start | bytes 294916
  20.8 4.8 %copy-start.9 = (bf16[384,512]{1,0:T(8,128)(2,1)S(1)}, bf16[384,512]{1,0:T(8,128)(2,1)}, u32[]{:S(2)}) copy-start(bf16[384,512]{1,0:T(8,128)(2,1)} %param.13) | copy-start | bytes 1179652
  20.8 33.4 %all-to-all-start.1 = ((bf16[8,152,512]{2,1,0:T(8,128)(2,1)}), bf16[8,152,512]{2,1,0:T(8,128)(2,1)}, u32[]{:S(2)}, u32[]{:S(2)}) async-start(bf16[8,152,512]{2,1,0:T(8,128)(2,1)} %bitcast.2), calls=%async_computation.1 | async-start | bytes 2490368 | tf_op jit(solution)/shard_map/all_to_all | solution.py:116
  26.5 109.6 %collective-permute-start = (s32[1,8,152]{2,1,0:T(8,128)}, s32[1,8,152]{2,1,0:T(8,128)}, u32[]{:S(2)}, u32[]{:S(2)}) collective-permute-start(s32[1,8,152]{2,1,0:T(8,128)} %fusion.137), channel_id=1, source_target_pairs={{0,1},{1,0},{2,3},{3,2},{4,5},{5,4},{6,7},{7,6},{8,9},{9,8},{10,11... | collective-permute-start | bytes 14600 | tf_op jit(solution)/shard_map/ppermute | solution.py:26
  56.8 1.4 copy-start.6
  58.2 1.3 copy-start.8
  59.5 1.0 copy-start.11
  59.5 1.6 copy-start.5
  69.5 2.5 %collective-permute-start.2 = (bf16[2,8,208,128]{3,2,1,0:T(8,128)(2,1)S(1)}, bf16[2,8,208,128]{3,2,1,0:T(8,128)(2,1)S(1)}, u32[]{:S(2)}, u32[]{:S(2)}) collective-permute-start(bf16[2,8,208,128]{3,2,1,0:T(8,128)(2,1)S(1)} %maximum_maximum_fusion.1), channel_id=1, source_target_pairs={{0,1},{1,0},{2,3},{3,2},{4,5},{5,4},{6,7},{7,6},{8,9},{9,8},{10,11... | collective-permute-start | bytes 2555912 | tf_op jit(solution)/shard_map/ppermute | solution.py:26
  72.2 12.3 %collective-permute-start.3 = (bf16[1,8,208,128]{3,2,1,0:T(8,128)(2,1)S(1)}, bf16[1,8,208,128]{3,2,1,0:T(8,128)(2,1)S(1)}, u32[]{:S(2)}, u32[]{:S(2)}) collective-permute-start(bf16[1,8,208,128]{3,2,1,0:T(8,128)(2,1)S(1)} %fusion.27), channel_id=1, source_target_pairs={{0,2},{1,3},{2,0},{3,1},{4,6},{5,7},{6,4},{7,5},{8,10},{9,11},{10,... | collective-permute-start | bytes 1277960 | tf_op jit(solution)/shard_map/ppermute | solution.py:26
  73.9 17.7 %collective-permute-start.9 = (bf16[2,8,64,768]{3,2,1,0:T(8,128)(2,1)S(1)}, bf16[2,8,64,768]{3,2,1,0:T(8,128)(2,1)S(1)}, u32[]{:S(2)}, u32[]{:S(2)}) collective-permute-start(bf16[2,8,64,768]{3,2,1,0:T(8,128)(2,1)S(1)} %maximum_maximum_fusion), channel_id=1, source_target_pairs={{0,1},{1,0},{2,3},{3,2},{4,5},{5,4},{6,7},{7,6},{8,9},{9,8},{10,11... | collective-permute-start | bytes 4718600 | tf_op jit(solution)/shard_map/ppermute | solution.py:26
  84.7 6.9 %collective-permute-start.4 = (bf16[4,208,128]{2,1,0:T(8,128)(2,1)S(1)}, bf16[4,208,128]{2,1,0:T(8,128)(2,1)S(1)}, u32[]{:S(2)}, u32[]{:S(2)}) collective-permute-start(bf16[4,208,128]{2,1,0:T(8,128)(2,1)S(1)} %fusion.61), channel_id=1, source_target_pairs={{0,4},{4,0},{8,12},{12,8},{16,20},{20,16},{24,28},{28,24},{1,5},{5... | collective-permute-start | bytes 638984 | tf_op jit(solution)/shard_map/ppermute | solution.py:26
  91.6 3.0 %copy-start.3 = (f32[4,208,128]{2,1,0:T(8,128)}, f32[4,208,128]{2,1,0:T(8,128)S(1)}, u32[]{:S(2)}) copy-start(f32[4,208,128]{2,1,0:T(8,128)S(1)} %fusion.47) | copy-start | bytes 1277956
  91.6 1.5 copy-start.7
  93.1 27.3 %collective-permute-start.10 = (bf16[1,8,64,768]{3,2,1,0:T(8,128)(2,1)}, bf16[1,8,64,768]{3,2,1,0:T(8,128)(2,1)}, u32[]{:S(2)}, u32[]{:S(2)}) collective-permute-start(bf16[1,8,64,768]{3,2,1,0:T(8,128)(2,1)} %fusion.11), channel_id=1, source_target_pairs={{0,2},{1,3},{2,0},{3,1},{4,6},{5,7},{6,4},{7,5},{8,10},{9,11},{10,... | collective-permute-start | bytes 2359304 | tf_op jit(solution)/shard_map/ppermute | solution.py:26
  94.6 8.8 %collective-permute-start.5 = (bf16[2,208,128]{2,1,0:T(8,128)(2,1)S(1)}, bf16[2,208,128]{2,1,0:T(8,128)(2,1)S(1)}, u32[]{:S(2)}, u32[]{:S(2)}) collective-permute-start(bf16[2,208,128]{2,1,0:T(8,128)(2,1)S(1)} %fusion.68), channel_id=1, source_target_pairs={{0,8},{4,12},{8,0},{12,4},{16,24},{20,28},{24,16},{28,20},{1,9},{5... | collective-permute-start | bytes 319496 | tf_op jit(solution)/shard_map/ppermute | solution.py:26
  99.9 3.6 %copy-start.4 = (f32[4,208,128]{2,1,0:T(8,128)S(1)}, f32[4,208,128]{2,1,0:T(8,128)}, u32[]{:S(2)}) copy-start(f32[4,208,128]{2,1,0:T(8,128)} %copy-done.3) | copy-start | bytes 1277956
  99.9 56.0 %all-to-all-start.2 = ((bf16[32,152,128]{2,1,0:T(8,128)(2,1)}), bf16[32,152,128]{2,1,0:T(8,128)(2,1)}, u32[]{:S(2)}, u32[]{:S(2)}) async-start(bf16[32,152,128]{2,1,0:T(8,128)(2,1)} %bitcast.5), calls=%async_computation.2 | async-start | bytes 2490368 | tf_op jit(solution)/shard_map/all_to_all | solution.py:147
  103.5 18.4 %copy-start.1 = (f32[512,384]{1,0:T(8,128)S(1)}, f32[512,384]{1,0:T(8,128)}, u32[]{:S(2)}) copy-start(f32[512,384]{1,0:T(8,128)} %convolution_multiply_fusion.11) | copy-start | bytes 2359300
  103.5 18.4 %copy-start.2 = (f32[512,384]{1,0:T(8,128)S(1)}, f32[512,384]{1,0:T(8,128)}, u32[]{:S(2)}) copy-start(f32[512,384]{1,0:T(8,128)} %convolution_multiply_fusion.10) | copy-start | bytes 2359300
  103.5 32.5 %collective-permute-start.6 = (bf16[1,208,128]{2,1,0:T(8,128)(2,1)S(1)}, bf16[1,208,128]{2,1,0:T(8,128)(2,1)S(1)}, u32[]{:S(2)}, u32[]{:S(2)}) collective-permute-start(bf16[1,208,128]{2,1,0:T(8,128)(2,1)S(1)} %fusion.79), channel_id=1, source_target_pairs={{0,16},{4,20},{8,24},{12,28},{16,0},{20,4},{24,8},{28,12},{1,17},{... | collective-permute-start | bytes 159752 | tf_op jit(solution)/shard_map/ppermute | solution.py:26
  122.2 16.8 %collective-permute-start.11 = (bf16[4,64,768]{2,1,0:T(8,128)(2,1)S(1)}, bf16[4,64,768]{2,1,0:T(8,128)(2,1)S(1)}, u32[]{:S(2)}, u32[]{:S(2)}) collective-permute-start(bf16[4,64,768]{2,1,0:T(8,128)(2,1)S(1)} %fusion.48), channel_id=1, source_target_pairs={{0,4},{4,0},{8,12},{12,8},{16,20},{20,16},{24,28},{28,24},{1,5},{5... | collective-permute-start | bytes 1179656 | tf_op jit(solution)/shard_map/ppermute | solution.py:26
  136.0 2.4 %collective-permute-start.7 = (bf16[1,208,128]{2,1,0:T(8,128)(2,1)S(1)}, bf16[1,208,128]{2,1,0:T(8,128)(2,1)S(1)}, u32[]{:S(2)}, u32[]{:S(2)}) collective-permute-start(bf16[1,208,128]{2,1,0:T(8,128)(2,1)S(1)} %fusion.69), channel_id=1, source_target_pairs={{0,1},{1,0},{2,3},{3,2},{4,5},{5,4},{6,7},{7,6},{8,9},{9,8},{10,11... | collective-permute-start | bytes 159752 | tf_op jit(solution)/shard_map/ppermute | solution.py:26
  136.9 3.7 %collective-permute-start.1 = (s32[2,8,152]{2,1,0:T(8,128)S(1)}, s32[2,8,152]{2,1,0:T(8,128)S(1)}, u32[]{:S(2)}, u32[]{:S(2)}) collective-permute-start(s32[2,8,152]{2,1,0:T(8,128)S(1)} %add_select_fusion.1), channel_id=1, source_target_pairs={{0,2},{1,3},{2,0},{3,1},{4,6},{5,7},{6,4},{7,5},{8,10},{9,11},{10,... | collective-permute-start | bytes 29192 | tf_op jit(solution)/shard_map/ppermute | solution.py:26
  138.4 5.1 %collective-permute-start.8 = (bf16[2,208,128]{2,1,0:T(8,128)(2,1)S(1)}, bf16[2,208,128]{2,1,0:T(8,128)(2,1)S(1)}, u32[]{:S(2)}, u32[]{:S(2)}) collective-permute-start(bf16[2,208,128]{2,1,0:T(8,128)(2,1)S(1)} %maximum_select_fusion.3), channel_id=1, source_target_pairs={{0,2},{1,3},{2,0},{3,1},{4,6},{5,7},{6,4},{7,5},{8,10},{9,11},{10,... | collective-permute-start | bytes 319496 | tf_op jit(solution)/shard_map/ppermute | solution.py:26
  139.2 6.8 %collective-permute-start.12 = (bf16[2,64,768]{2,1,0:T(8,128)(2,1)S(1)}, bf16[2,64,768]{2,1,0:T(8,128)(2,1)S(1)}, u32[]{:S(2)}, u32[]{:S(2)}) collective-permute-start(bf16[2,64,768]{2,1,0:T(8,128)(2,1)S(1)} %fusion.66), channel_id=1, source_target_pairs={{0,8},{4,12},{8,0},{12,4},{16,24},{20,28},{24,16},{28,20},{1,9},{5... | collective-permute-start | bytes 589832 | tf_op jit(solution)/shard_map/ppermute | solution.py:26
  146.1 6.8 %collective-permute-start.13 = (bf16[1,64,768]{2,1,0:T(8,128)(2,1)S(1)}, bf16[1,64,768]{2,1,0:T(8,128)(2,1)S(1)}, u32[]{:S(2)}, u32[]{:S(2)}) collective-permute-start(bf16[1,64,768]{2,1,0:T(8,128)(2,1)S(1)} %fusion.70), channel_id=1, source_target_pairs={{0,16},{4,20},{8,24},{12,28},{16,0},{20,4},{24,8},{28,12},{1,17},{... | collective-permute-start | bytes 294920 | tf_op jit(solution)/shard_map/ppermute | solution.py:26
  153.0 1.4 collective-permute-start.14
  154.4 10.0 %collective-permute-start.15 = (bf16[2,64,768]{2,1,0:T(8,128)(2,1)S(1)}, bf16[2,64,768]{2,1,0:T(8,128)(2,1)S(1)}, u32[]{:S(2)}, u32[]{:S(2)}) collective-permute-start(bf16[2,64,768]{2,1,0:T(8,128)(2,1)S(1)} %maximum_select_fusion.2), channel_id=1, source_target_pairs={{0,2},{1,3},{2,0},{3,1},{4,6},{5,7},{6,4},{7,5},{8,10},{9,11},{10,... | collective-permute-start | bytes 589832 | tf_op jit(solution)/shard_map/ppermute | solution.py:26

commit v2 on v1

--- a/solution.py
+++ b/solution.py
@@ -47,30 +47,102 @@
     return inputs, pre_hidden, hidden, message, upstream * update, d_gate_in, d_gate_mem
 
 
-def scatter_kernel(block, idx_ref, val_ref, out_ref):
-    rows = pl.program_id(0) * block + lax.broadcasted_iota(jnp.int32, (block, idx_ref.shape[1]), 0)
-    pick = jnp.where(rows == idx_ref[...], 1.0, 0.0).astype(BF16)
-    out_ref[...] = jnp.dot(pick, val_ref[...], preferred_element_type=F32)
+def scatter_kernel(low, idx_ref, idx_col_ref, val_ref, out_ref):
+    count, width = val_ref.shape
+    groups = out_ref.shape[0] // low
+    lows = lax.broadcasted_iota(jnp.int32, (low, count), 0)
+    pick = jnp.where(lows == idx_ref[...] % low, 1.0, 0.0).astype(BF16)
+    group = jnp.broadcast_to(idx_col_ref[...] // low, (count, width))
+    values = val_ref[...]
+    zero = jnp.zeros_like(values)
+    spread = jnp.concatenate([jnp.where(group == g, values, zero) for g in range(groups)], axis=1)
+    total = jnp.dot(pick, spread, preferred_element_type=F32)
+    for g in range(groups):
+        out_ref[pl.ds(g * low, low), :] = total[:, g * width : (g + 1) * width]
 
 
 def scatter_rows(index, values, rows):
     count, width = values.shape
-    block = 256
+    groups = 4
     return pl.pallas_call(
-        functools.partial(scatter_kernel, block),
+        functools.partial(scatter_kernel, rows // groups),
         out_shape=jax.ShapeDtypeStruct((rows, width), F32),
-        grid=(rows // block,),
+        cost_estimate=pl.CostEstimate(
+            flops=2 * rows * count * width,
+            bytes_accessed=count * width * 2 + rows * width * 4,
+            transcendentals=0,
+        ),
+    )(index.reshape(1, count), index.reshape(count, 1), values)
+
+
+def outgoing_kernel(slot_ref, grad_ref, out_ref):
+    parts, slots, part = out_ref.shape
+    count = slot_ref.shape[1]
+    rows = pl.program_id(0) * slots + lax.broadcasted_iota(jnp.int32, (slots, count), 0)
+    pick = jnp.where(rows == slot_ref[...], 1.0, 0.0).astype(BF16)
+    total = jnp.dot(pick, grad_ref[...], preferred_element_type=F32).astype(BF16)
+    for f in range(parts):
+        out_ref[f] = total[:, f * part : (f + 1) * part]
+
+
+def outgoing_rows(slot, grads, owners, slots, replicas):
+    count, width = grads.shape
+    part = width // replicas
+    return pl.pallas_call(
+        outgoing_kernel,
+        out_shape=jax.ShapeDtypeStruct((owners * replicas, slots, part), BF16),
+        grid=(owners,),
         in_specs=[
             pl.BlockSpec((1, count), lambda i: (0, 0)),
             pl.BlockSpec((count, width), lambda i: (0, 0)),
         ],
-        out_specs=pl.BlockSpec((block, width), lambda i: (i, 0)),
+        out_specs=pl.BlockSpec((replicas, slots, part), lambda i: (i, 0, 0)),
         cost_estimate=pl.CostEstimate(
-            flops=2 * rows * count * width,
-            bytes_accessed=count * width * 2 + rows * width * 4,
+            flops=2 * owners * slots * count * width,
+            bytes_accessed=(count + owners * slots) * width * 2,
             transcendentals=0,
         ),
-    )(index.reshape(1, count), values)
+    )(slot.reshape(1, count), grads)
+
+
+def weight_kernel(scale, count, which_ref, *refs):
+    out_ref = refs[-1]
+    lane = out_ref.shape[-1]
+    at = 0
+    for pair in range(count):
+        left, right = refs[2 * pair], refs[2 * pair + 1]
+        product = scale * contract_first(left[...], right[...])
+        for j in range(right.shape[1] // lane):
+            out_ref[0, at] = product[:, j * lane : (j + 1) * lane].astype(out_ref.dtype)
+            at += 1
+
+
+def weight_parts(pairs, which, replicas, lane, scale, dtype):
+    rows = pairs[0][0].shape[1]
+    tiles = sum(right.shape[1] // replicas // lane for _, right in pairs)
+    specs, args, flops = [], [], 0
+    for left, right in pairs:
+        cols = right.shape[1] // replicas
+        specs.append(pl.BlockSpec(left.shape, lambda i, w: (0, 0)))
+        specs.append(pl.BlockSpec((right.shape[0], cols), lambda i, w: (0, w[i])))
+        args += [left, right]
+        flops += 2 * left.shape[0] * rows * cols
+    number = which.shape[0]
+    return pl.pallas_call(
+        functools.partial(weight_kernel, scale, len(pairs)),
+        out_shape=jax.ShapeDtypeStruct((number, tiles, rows, lane), dtype),
+        grid_spec=pltpu.PrefetchScalarGridSpec(
+            num_scalar_prefetch=1,
+            grid=(number,),
+            in_specs=specs,
+            out_specs=pl.BlockSpec((1, tiles, rows, lane), lambda i, w: (i, 0, 0, 0)),
+        ),
+        cost_estimate=pl.CostEstimate(
+            flops=flops * number,
+            bytes_accessed=number * tiles * rows * lane * jnp.dtype(dtype).itemsize,
+            transcendentals=0,
+        ),
+    )(which, *args)
 
 
 def per_device(
@@ -142,91 +214,81 @@
     end_grads = jnp.concatenate([d_source, d_inputs[:, width:]], axis=0).astype(BF16)
 
     part = width // replicas
-    outgoing = contract_first(pick, end_grads).astype(BF16)
-    outgoing = outgoing.reshape(owners, slots, replicas, part).transpose(0, 2, 1, 3)
-    returned = lax.all_to_all(
-        outgoing.reshape(owners * replicas, slots, part), ("ent", "rep"), 0, 0, tiled=True
-    )
-    memory_grad = scatter_rows(index, returned.reshape(-1, part), ent_rows)
-
-    def quarter(pairs, which):
-        pieces = []
-        for left, right in pairs:
-            cols = right.shape[1] // replicas
-            piece = lax.dynamic_slice_in_dim(right, which * cols, cols, axis=1)
-            pieces.append(
-                (grad_scale * contract_first(left, piece)).reshape(owners, left.shape[1] // owners, cols)
-            )
-        return pieces
-
-    def halve_rep(make):
-        total = None
-        pending = [jnp.int32(0)]
-        flips = [0]
-        arrived = None
-        for bit in range(rep_bits):
-            later = [f for f in range(replicas) if f & (1 << bit) and not f & ((1 << bit) - 1)]
-            send = []
-            for flip in later:
-                value = make(rep ^ flip)
-                if arrived is not None:
-                    value = value + arrived[flip].astype(F32)
-                send.append(value.astype(BF16))
-            got = swap_bit(jnp.stack(send), "rep", bit)
-            fresh = {}
-            for place_, flip in enumerate(later):
-                base = flip ^ (1 << bit)
-                value = got[place_].astype(F32)
-                if arrived is not None:
-                    value = value + arrived[base]
-                fresh[base] = value
-            arrived = fresh
-        return make(rep) + arrived[0]
-
-    def halve_ent(value):
-        for bit in range(ent_bits):
-            upper = (ent >> bit) & 1
-            shape = value.shape
-            pairs = value.reshape((shape[0] // 2, 2) + shape[1:])
-            keep = jnp.where(upper == 1, pairs[:, 1], pairs[:, 0])
-            send = jnp.where(upper == 1, pairs[:, 0], pairs[:, 1]).astype(BF16)
-            value = keep + swap_bit(send, "ent", bit).astype(F32)
-        return value[0]
-
-    def spread_rep(value):
-        value = value.astype(BF16)[None]
-        for bit in range(rep_bits):
-            other = swap_bit(value, "rep", bit)
-            upper = (rep >> bit) & 1
-            value = jnp.where(
-                upper == 1,
-                jnp.concatenate([other, value], axis=0),
-                jnp.concatenate([value, other], axis=0),
-            )
-        return value.astype(F32)
-
-    def make_gate(which):
-        return jnp.concatenate(
-            quarter(((message, d_gate_in), (mem_src, d_gate_mem)), which), axis=2
-        )
-
-    def make_first(which):
-        return jnp.concatenate(quarter(((inputs, d_pre), (hidden, d_message)), which), axis=1)
-
-    gate_sum = spread_rep(halve_ent(halve_rep(make_gate)))
-    first_sum = spread_rep(halve_ent(halve_rep(make_first)))
-
-    def columns(value):
-        return jnp.transpose(value, (1, 0, 2)).reshape(value.shape[1], -1)
-
+    outgoing = outgoing_rows(slot, end_grads, owners, slots, replicas)
+    outgoing, d_message, d_pre = lax.optimization_barrier((outgoing, d_message, d_pre))
+    returned = lax.all_to_all(outgoing, ("ent", "rep"), 0, 0, tiled=True)
+    memory_grad = scatter_rows(index, returned.reshape(-1, width // replicas), ent_rows)
+
+    keep_first = [f for f in range(replicas) if not f & 1]
+    mine = rep ^ jnp.array(keep_first, jnp.int32)
+
+    def start(pairs):
+        send = weight_parts(pairs, mine ^ 1, replicas, part, grad_scale, BF16)
+        return swap_bit(send, "rep", 0)
+
+    def finish(pairs, arrived, order):
+        value = weight_parts(pairs, mine, replicas, part, grad_scale, F32) + arrived.astype(F32)
+        number, tiles, rows, lane = value.shape
+        value = value.reshape((2,) * (rep_bits - 1) + (tiles,) + (2,) * ent_bits + (rows // owners, lane))
+        left_rep = list(range(rep_bits - 1, 0, -1))
+        left_ent = list(range(ent_bits - 1, -1, -1))
+        for axis, bit in order:
+            if axis == "rep":
+                dim = left_rep.index(bit)
+                left_rep.remove(bit)
+                keep_at, send_at = jnp.int32(0), jnp.int32(1)
+            else:
+                dim = len(left_rep) + 1 + left_ent.index(bit)
+                left_ent.remove(bit)
+                keep_at = (ent >> bit) & 1
+                send_at = 1 - keep_at
+            send = lax.dynamic_index_in_dim(value, send_at, dim, keepdims=False).astype(BF16)
+            keep = lax.dynamic_index_in_dim(value, keep_at, dim, keepdims=False)
+            value = keep + swap_bit(send, axis, bit).astype(F32)
+        return value.reshape(-1, lane)
+
+    def rest(axis, bits, taken):
+        return [(axis, b) for b in range(bits) if (axis, b) not in taken]
+
+    def order_of(*head):
+        taken = set(head) | {("rep", 0)}
+        return list(head) + rest("rep", rep_bits, taken) + rest("ent", ent_bits, taken)
+
+    pairs_in = ((message, d_gate_in),)
+    pairs_mem = ((mem_src, d_gate_mem), (hidden, d_message))
+    pairs_first = ((inputs, d_pre),)
+    arrived_in = start(pairs_in)
+    arrived_mem = start(pairs_mem)
+    arrived_first = start(pairs_first)
+    sum_in = finish(pairs_in, arrived_in, order_of(("rep", rep_bits - 1)))
+    sum_mem = finish(pairs_mem, arrived_mem, order_of(("ent", 0)))
+    sum_first = finish(pairs_first, arrived_first, order_of(("ent", 1)))
+
+    value = jnp.concatenate([sum_first, sum_mem, sum_in], axis=0).astype(BF16)[None]
+    for bit in range(rep_bits - 1, -1, -1):
+        other = swap_bit(value, "rep", bit)
+        upper = (rep >> bit) & 1
+        pair = jnp.where(upper == 1, jnp.stack([other, value]), jnp.stack([value, other]))
+        value = pair.reshape((-1,) + value.shape[1:])
+    lane = value.shape[-1]
+    value = value.reshape((2,) * rep_bits + value.shape[1:])
+    value = jnp.transpose(value, tuple(range(rep_bits - 1, -1, -1)) + (rep_bits, rep_bits + 1))
+    value = value.reshape((replicas,) + value.shape[rep_bits:]).astype(F32)
     first_rows = inputs.shape[1] // owners
-    gate_cols = 3 * width // replicas
+    rows = width // owners
+
+    def columns(at, tiles, height):
+        block = value[:, at : at + tiles * height].reshape(replicas, tiles, height, lane)
+        return jnp.transpose(block, (2, 0, 1, 3)).reshape(height, replicas * tiles * lane)
+
+    tiles = 3 * width // replicas // lane
+    small = width // replicas // lane
     return (
         memory_grad,
-        columns(first_sum[:, :first_rows]),
-        columns(first_sum[:, first_rows:]),
-        columns(gate_sum[:, :, :gate_cols]),
-        columns(gate_sum[:, :, gate_cols:]),
+        columns(0, small, first_rows),
+        columns(first_rows * small + tiles * rows, small, rows),
+        columns(first_rows * small + (tiles + small) * rows, tiles, rows),
+        columns(first_rows * small, tiles, rows),
     )
 
 

time: 167 us -> 176 us (1.054)
  Pallas kernels: 8.44 us -> 35.3 us
  waiting for transfers between devices: 78.7 us -> 55.9 us
  matrix products: 23.7 us -> 11 us
  starting transfers between devices: 20.8 us -> 31.2 us
  other arithmetic: 7.64 us -> 14.3 us
    pallas_call x1 -> x8, Pallas kernels: 8.44 us -> 35.3 us  [the longest x6 22.4 us: weight_parts(): pl.pallas_call(functools.partial(weight_kernel, scale, len(pairs)), out_s...]
    ppermute x16 -> x19, waiting for transfers between devices: 51 us -> 28.5 us  [swap_bit(): return lax.ppermute(value, axis, [(i, i ^ 1 << bit) for i in range(size)])]
    dot_general x17 -> x0, matrix products: 10.2 us -> none  [contract_first(): lax.dot_general(left, right, (((0,), (0,)), ((), ())), preferred_element_...]
    ppermute x16 -> x19, starting transfers between devices: 12.7 us -> 22.8 us  [swap_bit(): return lax.ppermute(value, axis, [(i, i ^ 1 << bit) for i in range(size)])]
    concatenate x1 -> x4, other arithmetic: 0.21 us -> 4.55 us  [the longest x1 2.59 us: forward_gates(): jnp.concatenate([pre_reset, pre_update, pre_cand * reset_gate], axis=1)]
    add x6 -> x12, other arithmetic: 2.13 us -> 5.89 us  [the longest x3 4.29 us: finish(): weight_parts(pairs, mine, replicas, part, grad_scale, F32)]
    reshape x5 -> x2, local copies, waits for them, and re-layouts: 5.57 us -> 1.91 us  [columns(): jnp.transpose(block, (2, 0, 1, 3)).reshape(height, replicas * tiles * lane)]
    another operation x0 -> x1, local copies, waits for them, and re-layouts: none -> 2.21 us  [scatter_rows(): index.reshape(count, 1)]
  transfers between devices with their start and end apart: 18 -> 21, of which waited for: 10 -> 10; matrix products, arithmetic and copies ran while one was open for 20% -> 8% of each run, Pallas kernels for 5% -> 15%
where the time goes in v2:
time: 176 us; the launch traced here: 175 us
  waiting for transfers between devices  55.9 us (32%)
  Pallas kernels  35.3 us (20%)
  starting transfers between devices  31.2 us (18%)
  other arithmetic  14.3 us (8%)
  blocking collectives  13.6 us (8%)
  local copies, waits for them, and re-layouts  12.7 us (7%)
  matrix products  11 us (6%)
    ppermute x19, waiting for transfers between devices, swap_bit(): return lax.ppermute(value, axis, [(i, i ^ 1 << bit) for i in range(size)])  28.5 us
    all_to_all x1, waiting for transfers between devices, per_device(): lax.all_to_all(found.reshape(owners, slots, width), 'ent', 0, 0, tiled=True)  27.4 us
    ppermute x19, starting transfers between devices, swap_bit(): return lax.ppermute(value, axis, [(i, i ^ 1 << bit) for i in range(size)])  22.8 us
    pallas_call x6, Pallas kernels, weight_parts(): pl.pallas_call(functools.partial(weight_kernel, scale, len(pairs)), out_s...  22.4 us
    all_to_all x1, blocking collectives, per_device(): lax.all_to_all(wanted.reshape(owners, 1, cap), 'ent', 0, 0, tiled=True)  13.6 us
    pallas_call x1, Pallas kernels, scatter_rows(): pl.pallas_call(functools.partial(scatter_kernel, rows // groups), out_sha...  7.6 us
    pallas_call x1, Pallas kernels, outgoing_rows(): pl.pallas_call(outgoing_kernel, out_shape=jax.ShapeDtypeStruct((owners *...  5.32 us
    unnamed x45, local copies, waits for them, and re-layouts  4.93 us
  transfers between devices with their start and end apart: 21, of which 10 were waited for; matrix products, arithmetic and copies ran while one was open for 8% of the time, Pallas kernels for 15%

profile of v2, /device:TPU:0, one launch (start us, length us, event | category | flops | bytes accessed | tf_op | source)
XLA Modules:
  0.0 175.4 jit_solution(11374721897544290170)
XLA Ops:
  3.1 13.6 %all_to_all.15 = s32[8,1,144]{2,1,0:T(1,128)S(1)} all-to-all(s32[8,1,144]{2,1,0:T(1,128)S(1)} %reshape.707), channel_id=1, replica_groups=mesh['ent'=8,'rep'=4] {'ent'}, dimensions={0} | all-to-all | bytes 9216 | tf_op jit(solution)/shard_map/all_to_all | solution.py:182
  16.9 3.9 %fusion.3 = bf16[1216,512]{1,0:T(8,128)(2,1)} fusion(bf16[2048,512]{1,0:T(8,128)(2,1)S(1)} %copy-done, s32[1216]{0:T(1024)S(1)} %eq.59), kind=kOutput, calls=%fused_computation.6 | convolution fusion | flops 2553249792 | bytes 3347200 | tf_op jit(solution)/shard_map/dot_general | solution.py:187
  20.8 3.9 %all-to-all-start.1 = ((bf16[8,152,512]{2,1,0:T(8,128)(2,1)}), bf16[8,152,512]{2,1,0:T(8,128)(2,1)S(1)}, u32[]{:S(2)}, u32[]{:S(2)}) async-start(bf16[8,152,512]{2,1,0:T(8,128)(2,1)} %bitcast.130), calls=%async_computation.1 | async-start | bytes 2490368 | tf_op jit(solution)/shard_map/all_to_all | solution.py:188
  25.9 27.4 %all-to-all-done.1 = bf16[8,152,512]{2,1,0:T(8,128)(2,1)S(1)} async-done(((bf16[8,152,512]{2,1,0:T(8,128)(2,1)}), bf16[8,152,512]{2,1,0:T(8,128)(2,1)S(1)}, u32[]{:S(2)}, u32[]{:S(2)}) %all-to-all-start.1) | async-done | bytes 1245216 | tf_op jit(solution)/shard_map/all_to_all | solution.py:188
  66.3 5.3 %shard_map.137 = bf16[32,152,128]{2,1,0:T(8,128)(2,1)} custom-call(s32[1,768]{1,0:T(1,128)} %fusion.51.slot_ref, bf16[768,512]{1,0:T(8,128)(2,1)} %pad_maximum_fusion.4.grad_ref), custom_call_target="tpu_custom_call" | custom-call | flops 956301312 | bytes 2031616 | tf_op jit(solution)/shard_map/pallas_call | solution.py:91
  71.6 3.7 %shard_map.140 = bf16[2,1,1152,128]{3,2,1,0:T(8,128)(2,1)} custom-call(s32[2]{0:T(128)} %broadcast_xor_fusion.which_ref, bf16[384,1152]{1,0:T(8,128)(2,1)} %pad_maximum_fusion.3.refs_0_, bf16[384,512]{1,0:T(8,128)(2,1)} %copy-done.7), custom_call_target="tpu_custom_call" | custom-call | flops 226492416 | bytes 589824 | tf_op jit(solution)/shard_map/pallas_call | solution.py:131
  75.8 2.6 %pad_maximum_fusion = (bf16[384,1536]{1,0:T(8,128)(2,1)}, bf16[384,1536]{1,0:T(8,128)(2,1)}) fusion(bf16[384,512]{1,0:T(8,128)(2,1)S(1)} %get-tuple-element.11, bf16[384,512]{1,0:T(8,128)(2,1)S(1)} %copy-done.13, bf16[384,512]{1,0:T(8,128)(2,1)S(1)} %get-tuple-element.16, bf16[384,512]{1,0:T(8,128)(2,1)} %copy-done.14), kind=kLoop, calls=%fused_computation.24 | loop fusion | flops 5308416 | bytes 3932160 | tf_op jit(solution)/shard_map/concatenate | solution.py:46
  78.4 3.5 %shard_map.144 = bf16[2,3,512,128]{3,2,1,0:T(8,128)(2,1)} custom-call(s32[2]{0:T(128)} %broadcast_xor_fusion.which_ref, bf16[384,512]{1,0:T(8,128)(2,1)} %copy-done.2, bf16[384,1536]{1,0:T(8,128)(2,1)} %get-tuple-element.21.refs_1_), custom_call_target="tpu_custom_call" | custom-call | flops 301989888 | bytes 786432 | tf_op jit(solution)/shard_map/pallas_call | solution.py:131
  82.4 3.7 %shard_map.139 = f32[2,1,1152,128]{3,2,1,0:T(8,128)} custom-call(s32[2]{0:T(128)} %multiply_xor_fusion.which_ref, bf16[384,1152]{1,0:T(8,128)(2,1)} %pad_maximum_fusion.3.refs_0_, bf16[384,512]{1,0:T(8,128)(2,1)} %copy-done.7), custom_call_target="tpu_custom_call" | custom-call | flops 226492416 | bytes 1179648 | tf_op jit(solution)/shard_map/pallas_call | solution.py:131
  86.1 1.5 convert_add_fusion.2
  88.4 3.9 %shard_map.142 = bf16[2,4,512,128]{3,2,1,0:T(8,128)(2,1)} custom-call(s32[2]{0:T(128)} %broadcast_xor_fusion.which_ref, bf16[384,512]{1,0:T(8,128)(2,1)} %copy-done.3, bf16[384,1536]{1,0:T(8,128)(2,1)} %get-tuple-element.20.refs_1_, bf16[384,512]{1,0:T(8,128)(2,1)} %copy-done.6, bf16[384,512]{1,0:T(8,128)(2,1)} %copy-done.11), custom_call_target="tpu_custom_call" | custom-call | flops 402653184 | bytes 1048576 | tf_op jit(solution)/shard_map/pallas_call | solution.py:131
  92.8 4.5 %all-to-all-start.2 = ((bf16[32,152,128]{2,1,0:T(8,128)(2,1)}), bf16[32,152,128]{2,1,0:T(8,128)(2,1)}, u32[]{:S(2)}, u32[]{:S(2)}) async-start(bf16[32,152,128]{2,1,0:T(8,128)(2,1)} %shard_map.137), calls=%async_computation.2 | async-start | bytes 2490368 | tf_op jit(solution)/shard_map/all_to_all | solution.py:219
  97.3 3.6 %shard_map.143 = f32[2,3,512,128]{3,2,1,0:T(8,128)} custom-call(s32[2]{0:T(128)} %multiply_xor_fusion.which_ref, bf16[384,512]{1,0:T(8,128)(2,1)} %copy-done.2, bf16[384,1536]{1,0:T(8,128)(2,1)} %get-tuple-element.21.refs_1_), custom_call_target="tpu_custom_call" | custom-call | flops 301989888 | bytes 1572864 | tf_op jit(solution)/shard_map/pallas_call | solution.py:131
  100.9 4.1 %shard_map.141 = f32[2,4,512,128]{3,2,1,0:T(8,128)} custom-call(s32[2]{0:T(128)} %multiply_xor_fusion.which_ref, bf16[384,512]{1,0:T(8,128)(2,1)} %copy-done.3, bf16[384,1536]{1,0:T(8,128)(2,1)} %get-tuple-element.20.refs_1_, bf16[384,512]{1,0:T(8,128)(2,1)} %copy-done.6, bf16[384,512]{1,0:T(8,128)(2,1)} %copy-done.11), custom_call_target="tpu_custom_call" | custom-call | flops 402653184 | bytes 2097152 | tf_op jit(solution)/shard_map/pallas_call | solution.py:131
  106.2 1.6 collective-permute-start.4
  109.7 6.0 %collective-permute-done.4 = bf16[1,2,2,144,128]{4,3,2,1,0:T(8,128)(2,1)S(1)} collective-permute-done((bf16[1,2,2,144,128]{4,3,2,1,0:T(8,128)(2,1)S(1)}, bf16[1,2,2,144,128]{4,3,2,1,0:T(8,128)(2,1)S(1)}, u32[]{:S(2)}, u32[]{:S(2)}) %collective-permute-start.4) | collective-permute-done | bytes 147488 | tf_op jit(solution)/shard_map/ppermute | solution.py:26
  115.8 1.7 collective-permute-start.5
  121.0 2.4 %collective-permute-start.8 = (bf16[2,4,2,2,64,128]{5,4,3,2,1,0:T(8,128)(2,1)S(1)}, bf16[2,4,2,2,64,128]{5,4,3,2,1,0:T(8,128)(2,1)S(1)}, u32[]{:S(2)}, u32[]{:S(2)}) collective-permute-start(bf16[2,4,2,2,64,128]{5,4,3,2,1,0:T(8,128)(2,1)S(1)} %fusion.29), channel_id=1, source_target_pairs={{0,4},{4,0},{8,12},{12,8},{16,20},{20,16},{24,28},{28,24},{1,5},{5... | collective-permute-start | bytes 1572872 | tf_op jit(solution)/shard_map/ppermute | solution.py:26
  123.4 5.6 %collective-permute-done.6 = bf16[1,144,128]{2,1,0:T(8,128)(2,1)S(1)} collective-permute-done((bf16[1,144,128]{2,1,0:T(8,128)(2,1)S(1)}, bf16[1,144,128]{2,1,0:T(8,128)(2,1)S(1)}, u32[]{:S(2)}, u32[]{:S(2)}) %collective-permute-start.6) | collective-permute-done | bytes 36896 | tf_op jit(solution)/shard_map/ppermute | solution.py:26
  129.2 1.5 collective-permute-start.14
  130.7 5.7 %collective-permute-done.8 = bf16[2,4,2,2,64,128]{5,4,3,2,1,0:T(8,128)(2,1)S(1)} collective-permute-done((bf16[2,4,2,2,64,128]{5,4,3,2,1,0:T(8,128)(2,1)S(1)}, bf16[2,4,2,2,64,128]{5,4,3,2,1,0:T(8,128)(2,1)S(1)}, u32[]{:S(2)}, u32[]{:S(2)}) %collective-permute-start.8) | collective-permute-done | bytes 524320 | tf_op jit(solution)/shard_map/ppermute | solution.py:26
  136.7 1.5 collective-permute-start.9
  138.7 2.7 %collective-permute-start.15 = (bf16[3,2,64,128]{3,2,1,0:T(8,128)(2,1)S(1)}, bf16[3,2,64,128]{3,2,1,0:T(8,128)(2,1)S(1)}, u32[]{:S(2)}, u32[]{:S(2)}) collective-permute-start(bf16[3,2,64,128]{3,2,1,0:T(8,128)(2,1)S(1)} %fusion.38), channel_id=1, source_target_pairs={{0,8},{4,12},{8,0},{12,4},{16,24},{20,28},{24,16},{28,20},{1,9},{5... | collective-permute-start | bytes 294920 | tf_op jit(solution)/shard_map/ppermute | solution.py:26
  141.3 1.8 %collective-permute-done.9 = bf16[4,2,2,64,128]{4,3,2,1,0:T(8,128)(2,1)S(1)} collective-permute-done((bf16[4,2,2,64,128]{4,3,2,1,0:T(8,128)(2,1)S(1)}, bf16[4,2,2,64,128]{4,3,2,1,0:T(8,128)(2,1)S(1)}, u32[]{:S(2)}, u32[]{:S(2)}) %collective-permute-start.9) | collective-permute-done | bytes 262176 | tf_op jit(solution)/shard_map/ppermute | solution.py:26
  143.2 2.7 %collective-permute-start.10 = (bf16[4,2,64,128]{3,2,1,0:T(8,128)(2,1)S(1)}, bf16[4,2,64,128]{3,2,1,0:T(8,128)(2,1)S(1)}, u32[]{:S(2)}, u32[]{:S(2)}) collective-permute-start(bf16[4,2,64,128]{3,2,1,0:T(8,128)(2,1)S(1)} %fusion.36), channel_id=1, source_target_pairs={{0,8},{4,12},{8,0},{12,4},{16,24},{20,28},{24,16},{28,20},{1,9},{5... | collective-permute-start | bytes 393224 | tf_op jit(solution)/shard_map/ppermute | solution.py:26
  146.0 2.1 %collective-permute-start.16 = (bf16[3,64,128]{2,1,0:T(8,128)(2,1)S(1)}, bf16[3,64,128]{2,1,0:T(8,128)(2,1)S(1)}, u32[]{:S(2)}, u32[]{:S(2)}) collective-permute-start(bf16[3,64,128]{2,1,0:T(8,128)(2,1)S(1)} %fusion.43), channel_id=1, source_target_pairs={{0,16},{4,20},{8,24},{12,28},{16,0},{20,4},{24,8},{28,12},{1,17},{... | collective-permute-start | bytes 147464 | tf_op jit(solution)/shard_map/ppermute | solution.py:26
  148.1 1.5 collective-permute-done.10
  149.6 2.2 %collective-permute-start.11 = (bf16[4,64,128]{2,1,0:T(8,128)(2,1)S(1)}, bf16[4,64,128]{2,1,0:T(8,128)(2,1)S(1)}, u32[]{:S(2)}, u32[]{:S(2)}) collective-permute-start(bf16[4,64,128]{2,1,0:T(8,128)(2,1)S(1)} %fusion.42), channel_id=1, source_target_pairs={{0,16},{4,20},{8,24},{12,28},{16,0},{20,4},{24,8},{28,12},{1,17},{... | collective-permute-start | bytes 196616 | tf_op jit(solution)/shard_map/ppermute | solution.py:26
  151.8 3.0 %collective-permute-done.11 = bf16[4,64,128]{2,1,0:T(8,128)(2,1)S(1)} collective-permute-done((bf16[4,64,128]{2,1,0:T(8,128)(2,1)S(1)}, bf16[4,64,128]{2,1,0:T(8,128)(2,1)S(1)}, u32[]{:S(2)}, u32[]{:S(2)}) %collective-permute-start.11) | collective-permute-done | bytes 65568 | tf_op jit(solution)/shard_map/ppermute | solution.py:26
  157.1 3.3 %collective-permute-done.1 = s32[2,8,152]{2,1,0:T(8,128)S(1)} collective-permute-done((s32[2,8,152]{2,1,0:T(8,128)S(1)}, s32[2,8,152]{2,1,0:T(8,128)S(1)}, u32[]{:S(2)}, u32[]{:S(2)}) %collective-permute-start.1) | collective-permute-done | bytes 9760 | tf_op jit(solution)/shard_map/ppermute | solution.py:26
  160.4 2.2 %reshape_reshape.8.idx_col_ref = s32[4864,1]{1,0:T(8,128)} reshape(s32[8,4,152]{2,1,0:T(4,128)S(1)} %copy.39) | data formatting | bytes 38912 | tf_op jit(solution)/shard_map/reshape;reshape | solution.py:75
  163.5 7.6 %shard_map.138 = f32[2048,128]{1,0:T(8,128)} custom-call(s32[1,4864]{1,0:T(1,128)} %reshape_reshape.6.idx_ref, s32[4864,1]{1,0:T(8,128)} %reshape_reshape.8.idx_col_ref, bf16[4864,128]{1,0:T(8,128)(2,1)} %bitcast.4.val_ref), custom_call_target="tpu_custom_call" | custom-call | flops 2550136832 | bytes 2293760 | tf_op jit(solution)/shard_map/pallas_call | solution.py:67
  (146 shorter events, 34.0 us)
Async XLA Ops:
  0.6 16.3 %copy-start = (bf16[2048,512]{1,0:T(8,128)(2,1)S(1)}, bf16[2048,512]{1,0:T(8,128)(2,1)}, u32[]{:S(2)}) copy-start(bf16[2048,512]{1,0:T(8,128)(2,1)} %param.10) | copy-start | bytes 6291460
  20.8 4.4 %copy-start.18 = (s32[384]{0:T(512)S(1)}, s32[384]{0:T(512)}, u32[]{:S(2)}) copy-start(s32[384]{0:T(512)} %param.12) | copy-start | bytes 4612
  20.8 4.4 %copy-start.19 = (s32[384]{0:T(512)S(1)}, s32[384]{0:T(512)}, u32[]{:S(2)}) copy-start(s32[384]{0:T(512)} %param.13) | copy-start | bytes 4612
  20.8 32.5 %all-to-all-start.1 = ((bf16[8,152,512]{2,1,0:T(8,128)(2,1)}), bf16[8,152,512]{2,1,0:T(8,128)(2,1)S(1)}, u32[]{:S(2)}, u32[]{:S(2)}) async-start(bf16[8,152,512]{2,1,0:T(8,128)(2,1)} %bitcast.130), calls=%async_computation.1 | async-start | bytes 2490368 | tf_op jit(solution)/shard_map/all_to_all | solution.py:188
  54.5 1.9 %copy-start.15 = (bf16[1152,512]{1,0:T(8,128)(2,1)S(1)}, bf16[1152,512]{1,0:T(8,128)(2,1)}, u32[]{:S(2)}) copy-start(bf16[1152,512]{1,0:T(8,128)(2,1)} %param.15) | copy-start | bytes 3538948
  54.6 2.6 %copy-start.3 = (bf16[384,512]{1,0:T(8,128)(2,1)}, bf16[384,512]{1,0:T(8,128)(2,1)S(1)}, u32[]{:S(2)}) copy-start(bf16[384,512]{1,0:T(8,128)(2,1)S(1)} %get-tuple-element.23.refs_0_) | copy-start | bytes 1179652
  62.0 2.4 %copy-start.12 = (bf16[384,512]{1,0:T(8,128)(2,1)}, bf16[384,512]{1,0:T(8,128)(2,1)S(1)}, u32[]{:S(2)}) copy-start(bf16[384,512]{1,0:T(8,128)(2,1)S(1)} %get-tuple-element.17) | copy-start | bytes 1179652
  71.6 4.2 %copy-start.13 = (bf16[384,512]{1,0:T(8,128)(2,1)S(1)}, bf16[384,512]{1,0:T(8,128)(2,1)}, u32[]{:S(2)}) copy-start(bf16[384,512]{1,0:T(8,128)(2,1)} %copy-done.12) | copy-start | bytes 1179652
  75.3 10.7 %collective-permute-start.2 = (bf16[2,1,1152,128]{3,2,1,0:T(8,128)(2,1)}, bf16[2,1,1152,128]{3,2,1,0:T(8,128)(2,1)}, u32[]{:S(2)}, u32[]{:S(2)}) collective-permute-start(bf16[2,1,1152,128]{3,2,1,0:T(8,128)(2,1)} %shard_map.140), channel_id=1, source_target_pairs={{0,1},{1,0},{2,3},{3,2},{4,5},{5,4},{6,7},{7,6},{8,9},{9,8},{10,11... | collective-permute-start | bytes 1769480 | tf_op jit(solution)/shard_map/ppermute | solution.py:26
  81.9 25.8 %collective-permute-start.12 = (bf16[2,3,512,128]{3,2,1,0:T(8,128)(2,1)}, bf16[2,3,512,128]{3,2,1,0:T(8,128)(2,1)}, u32[]{:S(2)}, u32[]{:S(2)}) collective-permute-start(bf16[2,3,512,128]{3,2,1,0:T(8,128)(2,1)} %shard_map.144), channel_id=1, source_target_pairs={{0,1},{1,0},{2,3},{3,2},{4,5},{5,4},{6,7},{7,6},{8,9},{9,8},{10,11... | collective-permute-start | bytes 2359304 | tf_op jit(solution)/shard_map/ppermute | solution.py:26
  88.4 16.7 %collective-permute-start.3 = (bf16[2,1,2,2,144,128]{5,4,3,2,0,1:T(8,128)(2,1)}, bf16[2,1,2,2,144,128]{5,4,3,2,0,1:T(8,128)(2,1)}, u32[]{:S(2)}, u32[]{:S(2)}) collective-permute-start(bf16[2,1,2,2,144,128]{5,4,3,2,0,1:T(8,128)(2,1)} %fusion.31), channel_id=1, source_target_pairs={{0,8},{4,12},{8,0},{12,4},{16,24},{20,28},{24,16},{28,20},{1,9},{5... | collective-permute-start | bytes 884744 | tf_op jit(solution)/shard_map/ppermute | solution.py:26
  88.4 67.9 %collective-permute-start = (s32[1,8,152]{2,1,0:T(8,128)S(1)}, s32[1,8,152]{2,1,0:T(8,128)S(1)}, u32[]{:S(2)}, u32[]{:S(2)}) collective-permute-start(s32[1,8,152]{2,1,0:T(8,128)S(1)} %fusion.76), channel_id=1, source_target_pairs={{0,1},{1,0},{2,3},{3,2},{4,5},{5,4},{6,7},{7,6},{8,9},{9,8},{10,11... | collective-permute-start | bytes 14600 | tf_op jit(solution)/shard_map/ppermute | solution.py:26
  92.3 25.2 %collective-permute-start.7 = (bf16[2,4,512,128]{3,2,1,0:T(8,128)(2,1)}, bf16[2,4,512,128]{3,2,1,0:T(8,128)(2,1)}, u32[]{:S(2)}, u32[]{:S(2)}) collective-permute-start(bf16[2,4,512,128]{3,2,1,0:T(8,128)(2,1)} %shard_map.142), channel_id=1, source_target_pairs={{0,1},{1,0},{2,3},{3,2},{4,5},{5,4},{6,7},{7,6},{8,9},{9,8},{10,11... | collective-permute-start | bytes 3145736 | tf_op jit(solution)/shard_map/ppermute | solution.py:26
  92.8 70.7 %all-to-all-start.2 = ((bf16[32,152,128]{2,1,0:T(8,128)(2,1)}), bf16[32,152,128]{2,1,0:T(8,128)(2,1)}, u32[]{:S(2)}, u32[]{:S(2)}) async-start(bf16[32,152,128]{2,1,0:T(8,128)(2,1)} %shard_map.137), calls=%async_computation.2 | async-start | bytes 2490368 | tf_op jit(solution)/shard_map/all_to_all | solution.py:219
  105.0 2.7 %copy-start.4 = (f32[2,3,512,128]{3,2,1,0:T(8,128)S(1)}, f32[2,3,512,128]{3,2,1,0:T(8,128)}, u32[]{:S(2)}) copy-start(f32[2,3,512,128]{3,2,1,0:T(8,128)} %shard_map.143) | copy-start | bytes 4718596
  106.2 9.6 %collective-permute-start.4 = (bf16[1,2,2,144,128]{4,3,2,1,0:T(8,128)(2,1)S(1)}, bf16[1,2,2,144,128]{4,3,2,1,0:T(8,128)(2,1)S(1)}, u32[]{:S(2)}, u32[]{:S(2)}) collective-permute-start(bf16[1,2,2,144,128]{4,3,2,1,0:T(8,128)(2,1)S(1)} %fusion.35), channel_id=1, source_target_pairs={{0,2},{1,3},{2,0},{3,1},{4,6},{5,7},{6,4},{7,5},{8,10},{9,11},{10,... | collective-permute-start | bytes 442376 | tf_op jit(solution)/shard_map/ppermute | solution.py:26
  109.1 6.7 %copy-start.5 = (f32[2,3,512,128]{3,2,1,0:T(8,128)}, f32[2,3,512,128]{3,2,1,0:T(8,128)S(1)}, u32[]{:S(2)}) copy-start(f32[2,3,512,128]{3,2,1,0:T(8,128)S(1)} %convert_add_fusion.1) | copy-start | bytes 4718596
  109.1 8.5 %copy-start.1 = (f32[2,4,512,128]{3,2,1,0:T(8,128)S(1)}, f32[2,4,512,128]{3,2,1,0:T(8,128)}, u32[]{:S(2)}) copy-start(f32[2,4,512,128]{3,2,1,0:T(8,128)} %shard_map.141) | copy-start | bytes 6291460
  109.1 19.9 %collective-permute-start.13 = (bf16[3,2,2,2,64,128]{5,4,3,2,1,0:T(8,128)(2,1)S(1)}, bf16[3,2,2,2,64,128]{5,4,3,2,1,0:T(8,128)(2,1)S(1)}, u32[]{:S(2)}, u32[]{:S(2)}) collective-permute-start(bf16[3,2,2,2,64,128]{5,4,3,2,1,0:T(8,128)(2,1)S(1)} %bitcast.138), channel_id=1, source_target_pairs={{0,2},{1,3},{2,0},{3,1},{4,6},{5,7},{6,4},{7,5},{8,10},{9,11},{10,... | collective-permute-start | bytes 1179656 | tf_op jit(solution)/shard_map/ppermute | solution.py:26
  115.8 4.4 %collective-permute-start.5 = (bf16[1,2,144,128]{3,2,1,0:T(8,128)(2,1)S(1)}, bf16[1,2,144,128]{3,2,1,0:T(8,128)(2,1)S(1)}, u32[]{:S(2)}, u32[]{:S(2)}) collective-permute-start(bf16[1,2,144,128]{3,2,1,0:T(8,128)(2,1)S(1)} %fusion.40), channel_id=1, source_target_pairs={{0,4},{4,0},{8,12},{12,8},{16,20},{20,16},{24,28},{28,24},{1,5},{5... | collective-permute-start | bytes 221192 | tf_op jit(solution)/shard_map/ppermute | solution.py:26
  119.0 10.0 %slice-start = ((f32[2,3,512,128]{3,2,1,0:T(8,128)}), f32[1,3,512,128]{3,2,1,0:T(8,128)S(1)}, s32[]{:S(2)}) async-start(f32[2,3,512,128]{3,2,1,0:T(8,128)} %copy-done.5), calls=%async_computation.3 | async-start | bytes 1572864 | tf_op jit(solution)/shard_map/jit(dynamic_index_in_dim)/dynamic_slice | solution.py:246
  120.3 8.7 %collective-permute-start.6 = (bf16[1,144,128]{2,1,0:T(8,128)(2,1)S(1)}, bf16[1,144,128]{2,1,0:T(8,128)(2,1)S(1)}, u32[]{:S(2)}, u32[]{:S(2)}) collective-permute-start(bf16[1,144,128]{2,1,0:T(8,128)(2,1)S(1)} %fusion.44), channel_id=1, source_target_pairs={{0,16},{4,20},{8,24},{12,28},{16,0},{20,4},{24,8},{28,12},{1,17},{... | collective-permute-start | bytes 110600 | tf_op jit(solution)/shard_map/ppermute | solution.py:26
  121.0 15.5 %collective-permute-start.8 = (bf16[2,4,2,2,64,128]{5,4,3,2,1,0:T(8,128)(2,1)S(1)}, bf16[2,4,2,2,64,128]{5,4,3,2,1,0:T(8,128)(2,1)S(1)}, u32[]{:S(2)}, u32[]{:S(2)}) collective-permute-start(bf16[2,4,2,2,64,128]{5,4,3,2,1,0:T(8,128)(2,1)S(1)} %fusion.29), channel_id=1, source_target_pairs={{0,4},{4,0},{8,12},{12,8},{16,20},{20,16},{24,28},{28,24},{1,5},{5... | collective-permute-start | bytes 1572872 | tf_op jit(solution)/shard_map/ppermute | solution.py:26
  129.2 9.4 %collective-permute-start.14 = (bf16[3,2,2,64,128]{4,3,2,1,0:T(8,128)(2,1)S(1)}, bf16[3,2,2,64,128]{4,3,2,1,0:T(8,128)(2,1)S(1)}, u32[]{:S(2)}, u32[]{:S(2)}) collective-permute-start(bf16[3,2,2,64,128]{4,3,2,1,0:T(8,128)(2,1)S(1)} %fusion.34), channel_id=1, source_target_pairs={{0,4},{4,0},{8,12},{12,8},{16,20},{20,16},{24,28},{28,24},{1,5},{5... | collective-permute-start | bytes 589832 | tf_op jit(solution)/shard_map/ppermute | solution.py:26
  136.7 6.4 %collective-permute-start.9 = (bf16[4,2,2,64,128]{4,3,2,1,0:T(8,128)(2,1)S(1)}, bf16[4,2,2,64,128]{4,3,2,1,0:T(8,128)(2,1)S(1)}, u32[]{:S(2)}, u32[]{:S(2)}) collective-permute-start(bf16[4,2,2,64,128]{4,3,2,1,0:T(8,128)(2,1)S(1)} %fusion.33), channel_id=1, source_target_pairs={{0,2},{1,3},{2,0},{3,1},{4,6},{5,7},{6,4},{7,5},{8,10},{9,11},{10,... | collective-permute-start | bytes 786440 | tf_op jit(solution)/shard_map/ppermute | solution.py:26
  138.7 7.3 %collective-permute-start.15 = (bf16[3,2,64,128]{3,2,1,0:T(8,128)(2,1)S(1)}, bf16[3,2,64,128]{3,2,1,0:T(8,128)(2,1)S(1)}, u32[]{:S(2)}, u32[]{:S(2)}) collective-permute-start(bf16[3,2,64,128]{3,2,1,0:T(8,128)(2,1)S(1)} %fusion.38), channel_id=1, source_target_pairs={{0,8},{4,12},{8,0},{12,4},{16,24},{20,28},{24,16},{28,20},{1,9},{5... | collective-permute-start | bytes 294920 | tf_op jit(solution)/shard_map/ppermute | solution.py:26
  143.2 6.3 %collective-permute-start.10 = (bf16[4,2,64,128]{3,2,1,0:T(8,128)(2,1)S(1)}, bf16[4,2,64,128]{3,2,1,0:T(8,128)(2,1)S(1)}, u32[]{:S(2)}, u32[]{:S(2)}) collective-permute-start(bf16[4,2,64,128]{3,2,1,0:T(8,128)(2,1)S(1)} %fusion.36), channel_id=1, source_target_pairs={{0,8},{4,12},{8,0},{12,4},{16,24},{20,28},{24,16},{28,20},{1,9},{5... | collective-permute-start | bytes 393224 | tf_op jit(solution)/shard_map/ppermute | solution.py:26
  146.0 5.8 %collective-permute-start.16 = (bf16[3,64,128]{2,1,0:T(8,128)(2,1)S(1)}, bf16[3,64,128]{2,1,0:T(8,128)(2,1)S(1)}, u32[]{:S(2)}, u32[]{:S(2)}) collective-permute-start(bf16[3,64,128]{2,1,0:T(8,128)(2,1)S(1)} %fusion.43), channel_id=1, source_target_pairs={{0,16},{4,20},{8,24},{12,28},{16,0},{20,4},{24,8},{28,12},{1,17},{... | collective-permute-start | bytes 147464 | tf_op jit(solution)/shard_map/ppermute | solution.py:26
  149.6 5.2 %collective-permute-start.11 = (bf16[4,64,128]{2,1,0:T(8,128)(2,1)S(1)}, bf16[4,64,128]{2,1,0:T(8,128)(2,1)S(1)}, u32[]{:S(2)}, u32[]{:S(2)}) collective-permute-start(bf16[4,64,128]{2,1,0:T(8,128)(2,1)S(1)} %fusion.42), channel_id=1, source_target_pairs={{0,16},{4,20},{8,24},{12,28},{16,0},{20,4},{24,8},{28,12},{1,17},{... | collective-permute-start | bytes 196616 | tf_op jit(solution)/shard_map/ppermute | solution.py:26
  154.9 8.4 %collective-permute-start.17 = (bf16[1,592,128]{2,1,0:T(8,128)(2,1)S(1)}, bf16[1,592,128]{2,1,0:T(8,128)(2,1)S(1)}, u32[]{:S(2)}, u32[]{:S(2)}) collective-permute-start(bf16[1,592,128]{2,1,0:T(8,128)(2,1)S(1)} %get-tuple-element.25), channel_id=1, source_target_pairs={{0,2},{1,3},{2,0},{3,1},{4,6},{5,7},{6,4},{7,5},{8,10},{9,11},{10,... | collective-permute-start | bytes 454664 | tf_op jit(solution)/shard_map/ppermute | solution.py:26
  156.4 4.0 %collective-permute-start.1 = (s32[2,8,152]{2,1,0:T(8,128)S(1)}, s32[2,8,152]{2,1,0:T(8,128)S(1)}, u32[]{:S(2)}, u32[]{:S(2)}) collective-permute-start(s32[2,8,152]{2,1,0:T(8,128)S(1)} %add_select_fusion.1), channel_id=1, source_target_pairs={{0,2},{1,3},{2,0},{3,1},{4,6},{5,7},{6,4},{7,5},{8,10},{9,11},{10,... | collective-permute-start | bytes 29192 | tf_op jit(solution)/shard_map/ppermute | solution.py:26
  163.4 7.7 %collective-permute-start.18 = (bf16[2,592,128]{2,1,0:T(8,128)(2,1)S(1)}, bf16[2,592,128]{2,1,0:T(8,128)(2,1)S(1)}, u32[]{:S(2)}, u32[]{:S(2)}) collective-permute-start(bf16[2,592,128]{2,1,0:T(8,128)(2,1)S(1)} %maximum_select_fusion.1), channel_id=1, source_target_pairs={{0,1},{1,0},{2,3},{3,2},{4,5},{5,4},{6,7},{7,6},{8,9},{9,8},{10,11... | collective-permute-start | bytes 909320 | tf_op jit(solution)/shard_map/ppermute | solution.py:26
  (10 other events, 10.3 us)
